TPU v7x, 256 devices: a whole 4x4x8 slice. The times are simulated.
256 devices in a mesh: tm: 64 (over y, x_lo, z), space: 4 (over x_hi, core).
Axes of the slice: x: 4 (x_hi: 2, x_lo: 2; x = x_hi * 2 + x_lo), y: 4, z: 8, core: 2. Of those that a mesh axis runs over, the one named last changes fastest.
Arguments:
- end_state: float32 [64, 5, 64, 1024], P('tm', None, None, 'space'), may hold values from -6 to 6
- forcing: bfloat16 [64, 2, 5, 64, 1024], P('tm', None, None, None, 'space'), may hold values from -3 to 3
- jacobians: float32 [64, 3, 5, 5, 1024], P('tm', None, None, None, 'space'), may hold values from -2.7 to 2.7
- coarse_blocks: float32 [64, 5, 5, 1024], P('tm', None, None, 'space'), as said below
- neighbors: int32 [6, 1024], P(None, 'space'), may hold values from 0 to 511, as said below
- orientation: int32 [6, 1024], P(None, 'space'), may hold values from 0 to 7
- interfaces: int32 [2, 512], P(None, 'space'), may hold values from 0 to 255, as said below
Outputs:
- new_end: float32 [64, 5, 64, 1024], P('tm', None, None, 'space')
Inputs may be any that keep to these rules, and one draw needn't show every extreme that they name: `neighbors`: entry [k, e] names the element across face k (-x, +x, -y, +y, -z, +z) of local element e of the same partition. Only -x faces of the partition's first layer hold 256 + s and only +x faces of its last layer hold 384 + s; s indexes row 1 of interfaces of the partition before, or row 0 of the partition after; y and z wrap inside a partition. `interfaces`: row 0 lists a partition's local elements whose -x face is its boundary, row 1 those whose +x face is, each ordered by position in y and z, so that slot s of row 1 faces slot s of row 0 of the next partition. `coarse_blocks`: one 5 x 5 block per interval and element.
All inputs are finite; a program needn't handle non-finite values.
Results may differ from a plain program's by a relative error of at most 0.0003.
Values sent between devices are 32-bit elements; how exact they have to be, the bound alone decides.
A program may use at most 64 MiB of HBM per device.

v0:
```python
import math

import jax
import jax.numpy as jnp
import numpy as np
from jax import lax
from jax.sharding import PartitionSpec as P

highest = lax.Precision.HIGHEST
step_size = 0.02
penalty = 0.5
lift_scale = 6.0


def shifted(block, axis, distance):
    devices = range(lax.axis_size(axis))
    route = [((i - distance) % len(devices), i) for i in devices]
    return lax.ppermute(block, axis, route)


def passed_along(value, axis, steps):
    count = lax.axis_size(axis)
    leading, last = (max(0, -steps), min(count, count - steps))
    return lax.ppermute(value, axis, [(source, source + steps) for source in range(leading, last)])


def tables():
    gll_nodes = np.array([-1.0, -math.sqrt(0.2), math.sqrt(0.2), 1.0])
    bary_weights = np.array(
        [1.0 / np.prod([gll_nodes[j] - gll_nodes[k] for k in range(4) if k != j]) for j in range(4)]
    )
    derivative = np.zeros((4, 4))
    for i in range(4):
        for j in range(4):
            if i != j:
                derivative[i, j] = bary_weights[j] / bary_weights[i] / (gll_nodes[i] - gll_nodes[j])
        derivative[i, i] = -derivative[i].sum()
    identity = np.eye(4)
    derivatives = np.stack(
        [
            np.kron(np.kron(derivative, identity), identity),
            np.kron(np.kron(identity, derivative), identity),
            np.kron(np.kron(identity, identity), derivative),
        ]
    )
    weights = np.array([1.0, 5.0, 5.0, 1.0]) / 6.0
    cube_weights = (
        weights[:, None, None] * weights[None, :, None] * weights[None, None, :]
    ).reshape(64) / 8.0
    node_grid = np.arange(64).reshape(4, 4, 4)
    face_nodes = np.stack(
        [
            node_grid[0].reshape(16),
            node_grid[3].reshape(16),
            node_grid[:, 0].reshape(16),
            node_grid[:, 3].reshape(16),
            node_grid[:, :, 0].reshape(16),
            node_grid[:, :, 3].reshape(16),
        ]
    )
    face_grid = np.arange(16).reshape(4, 4)
    orientations = []
    for symmetry in range(8):
        arranged = face_grid
        if symmetry & 4:
            arranged = arranged.T
        if symmetry & 2:
            arranged = arranged[::-1]
        if symmetry & 1:
            arranged = arranged[:, ::-1]
        orientations.append(arranged.reshape(16))
    orientations = np.stack(orientations)
    lift_maps = np.zeros((6, 64, 16))
    for k in range(6):
        lift_maps[k, face_nodes[k], np.arange(16)] = lift_scale
    return (
        jnp.asarray(derivatives, jnp.float32),
        jnp.asarray(cube_weights, jnp.float32),
        face_nodes,
        orientations,
        jnp.asarray(lift_maps, jnp.float32),
    )


def mix_fields(blocks, values):
    result = blocks[0][:, None] * values[0][None]
    for source in range(1, blocks.shape[0]):
        result = result + blocks[source][:, None] * values[source][None]
    return result


def reorient(fetched, orient_codes, orientations):
    result = jnp.zeros_like(fetched)
    for symmetry in range(8):
        result = result + jnp.where(
            orient_codes[None, None] == symmetry, fetched[:, orientations[symmetry]], 0.0
        )
    return result


def adjoint_step(adjoint, jacobian, forcing, neighbors, orientation, interfaces, statics):
    derivatives, cube_weights, face_nodes, orientations, lift_maps = statics
    traces = [adjoint[:, face_nodes[k]] for k in range(6)]
    left_part = jnp.take(traces[0], interfaces[0], axis=2)
    right_part = jnp.take(traces[1], interfaces[1], axis=2)
    from_left = shifted(right_part, "space", 1)
    from_right = shifted(left_part, "space", -1)
    volume = jnp.zeros_like(adjoint)
    for axis_num in range(3):
        mixed_terms = mix_fields(jacobian[axis_num], adjoint)
        volume = volume + jnp.einsum(
            "ji,fje->fie", derivatives[axis_num], mixed_terms, precision=highest
        )
    for k in range(6):
        across = jnp.concatenate([traces[k ^ 1], from_left, from_right], axis=2)
        fetched = jnp.take(across, neighbors[k], axis=2)
        aligned = reorient(fetched, orientation[k], orientations)
        trace_jump = aligned - traces[k]
        normal_sign = 0.5 if k % 2 == 1 else -0.5
        face_flux = normal_sign * mix_fields(jacobian[k // 2], trace_jump) + penalty * trace_jump
        volume = volume + jnp.einsum("ij,fje->fie", lift_maps[k], face_flux, precision=highest)
    return adjoint + step_size * volume + forcing.astype(jnp.float32)


def apply_block(coarse_map, vector):
    return jnp.sum(coarse_map * vector[None], axis=1)


def per_device(end_state, forcing, jacobians, coarse_blocks, neighbors, orientation, interfaces):
    statics = tables()
    cube_weights = statics[1]
    adjoint = end_state[0]
    start_state = adjoint_step(
        adjoint, jacobians[0], forcing[0, 1], neighbors, orientation, interfaces, statics
    )
    start_state = adjoint_step(
        start_state, jacobians[0], forcing[0, 0], neighbors, orientation, interfaces, statics
    )
    received = shifted(start_state, "tm", 1)
    residual = received - adjoint
    coarse_residual = jnp.einsum("fie,i->fe", residual, cube_weights, precision=highest)
    coarse_map = coarse_blocks[0]

    def relay_turn(turn_index, current):
        earlier_value = passed_along(current, "tm", 1)
        return coarse_residual + apply_block(coarse_map, earlier_value)

    correction = lax.fori_loop(0, lax.axis_size("tm") - 1, relay_turn, coarse_residual)
    return (adjoint + residual + correction[:, None, :])[None]


def solution(mesh):
    in_specs = (
        P("tm", None, None, "space"),
        P("tm", None, None, None, "space"),
        P("tm", None, None, None, "space"),
        P("tm", None, None, "space"),
        P(None, "space"),
        P(None, "space"),
        P(None, "space"),
    )
    out_specs = P("tm", None, None, "space")
    return jax.shard_map(
        per_device, mesh=mesh, in_specs=in_specs, out_specs=out_specs, check_vma=False
    )
```

profile of v0, /device:TPU:24, one launch (start us, length us, event | category | flops | bytes accessed | tf_op | source)
XLA Modules:
  0.0 819.4 jit_solution(16658234459599504511)
XLA Ops:
  263.9 12.2 %collective-permute-done.5 = f32[5,64,256]{2,1,0:T(8,128)S(1)} collective-permute-done((f32[5,64,256]{2,1,0:T(8,128)S(1)}, f32[5,64,256]{2,1,0:T(8,128)S(1)}, u32[]{:S(2)}, u32[]{:S(2)}) %collective-permute-start.5) | collective-permute-done | bytes 327712 | tf_op jit(solution)/shard_map/ppermute | solution.py:18
  276.4 542.0 %while.10 = (s32[]{:T(128)}, f32[5,256]{1,0:T(8,128)S(1)}, f32[5,5,256]{2,1,0:T(8,128)S(1)}, f32[5,256]{1,0:T(8,128)S(1)}, s32[]{:T(128)}) while((s32[]{:T(128)}, f32[5,256]{1,0:T(8,128)S(1)}, f32[5,5,256]{2,1,0:T(8,128)S(1)}, f32[5,256]{1,0:T(8,128)S(1)}, s32[]{:T(128)}) %tuple.216), condition=%wide.region_2.5_spmd, body=%wide.region_0.4_spmd.sunk | while | flops 12802 | bytes 71781 | solution.py:148
  278.4 6.6 collective-permute-done
  287.0 6.6 collective-permute-done
  295.6 6.6 collective-permute-done
  304.2 6.6 collective-permute-done
  312.8 6.6 collective-permute-done
  321.4 6.6 collective-permute-done
  347.2 6.6 collective-permute-done
  355.8 6.6 collective-permute-done
  364.4 6.6 collective-permute-done
  373.0 6.6 collective-permute-done
  381.6 6.6 collective-permute-done
  390.2 6.6 collective-permute-done
  398.8 6.6 collective-permute-done
  407.4 6.6 collective-permute-done
  424.6 6.6 collective-permute-done
  433.2 6.6 collective-permute-done
  441.8 6.6 collective-permute-done
  450.4 6.6 collective-permute-done
  459.0 6.6 collective-permute-done
  467.6 6.6 collective-permute-done
  476.2 6.6 collective-permute-done
  484.8 6.6 collective-permute-done
  510.6 6.6 collective-permute-done
  519.2 6.6 collective-permute-done
  527.8 6.6 collective-permute-done
  536.4 6.6 collective-permute-done
  545.0 6.6 collective-permute-done
  553.7 6.6 collective-permute-done
  562.3 6.6 collective-permute-done
  570.9 6.6 collective-permute-done
  588.1 6.6 collective-permute-done
  596.7 6.6 collective-permute-done
  605.3 6.6 collective-permute-done
  613.9 6.6 collective-permute-done
  622.5 6.6 collective-permute-done
  631.1 6.6 collective-permute-done
  639.7 6.6 collective-permute-done
  648.3 6.6 collective-permute-done
  674.1 6.6 collective-permute-done
  682.7 6.6 collective-permute-done
  691.3 6.6 collective-permute-done
  699.9 6.6 collective-permute-done
  708.5 6.6 collective-permute-done
  717.1 6.6 collective-permute-done
  725.7 6.6 collective-permute-done
  734.3 6.6 collective-permute-done
  (960 shorter events, 495.8 us)
Async XLA Ops:
  4.1 21.8 %collective-permute-start.2 = (f32[5,16,128]{2,0,1:T(8,128)S(1)}, f32[5,16,128]{2,0,1:T(8,128)S(1)}, u32[]{:S(2)}, u32[]{:S(2)}) collective-permute-start(f32[5,16,128]{2,0,1:T(8,128)S(1)} %select_bitcast_fusion.14), channel_id=1, source_target_pairs={{1,0},{2,1},{3,2},{0,3},{5,4},{6,5},{7,6},{4,7},{9,8},{10,9},{11,1... | collective-permute-start | bytes 122888 | tf_op jit(solution)/shard_map/ppermute | solution.py:18
  8.7 17.2 %collective-permute-start.1 = (f32[5,16,128]{2,0,1:T(8,128)S(1)}, f32[5,16,128]{2,0,1:T(8,128)S(1)}, u32[]{:S(2)}, u32[]{:S(2)}) collective-permute-start(f32[5,16,128]{2,0,1:T(8,128)S(1)} %select_bitcast_fusion.15), channel_id=1, source_target_pairs={{3,0},{0,1},{1,2},{2,3},{7,4},{4,5},{5,6},{6,7},{11,8},{8,9},{9,10... | collective-permute-start | bytes 122888 | tf_op jit(solution)/shard_map/ppermute | solution.py:18
  143.0 10.2 %collective-permute-start.4 = (f32[5,16,128]{2,0,1:T(8,128)}, f32[5,16,128]{2,0,1:T(8,128)}, u32[]{:S(2)}, u32[]{:S(2)}) collective-permute-start(f32[5,16,128]{2,0,1:T(8,128)} %select_bitcast_fusion.12), channel_id=1, source_target_pairs={{1,0},{2,1},{3,2},{0,3},{5,4},{6,5},{7,6},{4,7},{9,8},{10,9},{11,1... | collective-permute-start | bytes 122888 | tf_op jit(solution)/shard_map/ppermute | solution.py:18
  261.9 14.2 %collective-permute-start.5 = (f32[5,64,256]{2,1,0:T(8,128)S(1)}, f32[5,64,256]{2,1,0:T(8,128)S(1)}, u32[]{:S(2)}, u32[]{:S(2)}) collective-permute-start(f32[5,64,256]{2,1,0:T(8,128)S(1)} %fusion.19), channel_id=1, source_target_pairs={{252,0},{0,4},{4,8},{8,12},{12,16},{16,20},{20,24},{24,28},{28,32}... | collective-permute-start | bytes 983048 | tf_op jit(solution)/shard_map/ppermute | solution.py:18
  276.4 8.6 %collective-permute-start = (f32[5,256]{1,0:T(8,128)S(1)}, f32[5,256]{1,0:T(8,128)S(1)}, u32[]{:S(2)}, u32[]{:S(2)}) collective-permute-start(f32[5,256]{1,0:T(8,128)S(1)} %get-tuple-element.313), channel_id=1, source_target_pairs={{0,4},{4,8},{8,12},{12,16},{16,20},{20,24},{24,28},{28,32},{32,36}... | collective-permute-start | bytes 15368 | tf_op jit(solution)/shard_map/while/body/eval_jaxpr/ppermute | solution.py:24
  285.0 8.6 %collective-permute-start = (f32[5,256]{1,0:T(8,128)S(1)}, f32[5,256]{1,0:T(8,128)S(1)}, u32[]{:S(2)}, u32[]{:S(2)}) collective-permute-start(f32[5,256]{1,0:T(8,128)S(1)} %get-tuple-element.313), channel_id=1, source_target_pairs={{0,4},{4,8},{8,12},{12,16},{16,20},{20,24},{24,28},{28,32},{32,36}... | collective-permute-start | bytes 15368 | tf_op jit(solution)/shard_map/while/body/eval_jaxpr/ppermute | solution.py:24
  293.6 8.6 %collective-permute-start = (f32[5,256]{1,0:T(8,128)S(1)}, f32[5,256]{1,0:T(8,128)S(1)}, u32[]{:S(2)}, u32[]{:S(2)}) collective-permute-start(f32[5,256]{1,0:T(8,128)S(1)} %get-tuple-element.313), channel_id=1, source_target_pairs={{0,4},{4,8},{8,12},{12,16},{16,20},{20,24},{24,28},{28,32},{32,36}... | collective-permute-start | bytes 15368 | tf_op jit(solution)/shard_map/while/body/eval_jaxpr/ppermute | solution.py:24
  302.2 8.6 %collective-permute-start = (f32[5,256]{1,0:T(8,128)S(1)}, f32[5,256]{1,0:T(8,128)S(1)}, u32[]{:S(2)}, u32[]{:S(2)}) collective-permute-start(f32[5,256]{1,0:T(8,128)S(1)} %get-tuple-element.313), channel_id=1, source_target_pairs={{0,4},{4,8},{8,12},{12,16},{16,20},{20,24},{24,28},{28,32},{32,36}... | collective-permute-start | bytes 15368 | tf_op jit(solution)/shard_map/while/body/eval_jaxpr/ppermute | solution.py:24
  310.8 8.6 %collective-permute-start = (f32[5,256]{1,0:T(8,128)S(1)}, f32[5,256]{1,0:T(8,128)S(1)}, u32[]{:S(2)}, u32[]{:S(2)}) collective-permute-start(f32[5,256]{1,0:T(8,128)S(1)} %get-tuple-element.313), channel_id=1, source_target_pairs={{0,4},{4,8},{8,12},{12,16},{16,20},{20,24},{24,28},{28,32},{32,36}... | collective-permute-start | bytes 15368 | tf_op jit(solution)/shard_map/while/body/eval_jaxpr/ppermute | solution.py:24
  319.4 8.6 %collective-permute-start = (f32[5,256]{1,0:T(8,128)S(1)}, f32[5,256]{1,0:T(8,128)S(1)}, u32[]{:S(2)}, u32[]{:S(2)}) collective-permute-start(f32[5,256]{1,0:T(8,128)S(1)} %get-tuple-element.313), channel_id=1, source_target_pairs={{0,4},{4,8},{8,12},{12,16},{16,20},{20,24},{24,28},{28,32},{32,36}... | collective-permute-start | bytes 15368 | tf_op jit(solution)/shard_map/while/body/eval_jaxpr/ppermute | solution.py:24
  336.6 8.6 %collective-permute-start = (f32[5,256]{1,0:T(8,128)S(1)}, f32[5,256]{1,0:T(8,128)S(1)}, u32[]{:S(2)}, u32[]{:S(2)}) collective-permute-start(f32[5,256]{1,0:T(8,128)S(1)} %get-tuple-element.313), channel_id=1, source_target_pairs={{0,4},{4,8},{8,12},{12,16},{16,20},{20,24},{24,28},{28,32},{32,36}... | collective-permute-start | bytes 15368 | tf_op jit(solution)/shard_map/while/body/eval_jaxpr/ppermute | solution.py:24
  345.2 8.6 %collective-permute-start = (f32[5,256]{1,0:T(8,128)S(1)}, f32[5,256]{1,0:T(8,128)S(1)}, u32[]{:S(2)}, u32[]{:S(2)}) collective-permute-start(f32[5,256]{1,0:T(8,128)S(1)} %get-tuple-element.313), channel_id=1, source_target_pairs={{0,4},{4,8},{8,12},{12,16},{16,20},{20,24},{24,28},{28,32},{32,36}... | collective-permute-start | bytes 15368 | tf_op jit(solution)/shard_map/while/body/eval_jaxpr/ppermute | solution.py:24
  353.9 8.6 %collective-permute-start = (f32[5,256]{1,0:T(8,128)S(1)}, f32[5,256]{1,0:T(8,128)S(1)}, u32[]{:S(2)}, u32[]{:S(2)}) collective-permute-start(f32[5,256]{1,0:T(8,128)S(1)} %get-tuple-element.313), channel_id=1, source_target_pairs={{0,4},{4,8},{8,12},{12,16},{16,20},{20,24},{24,28},{28,32},{32,36}... | collective-permute-start | bytes 15368 | tf_op jit(solution)/shard_map/while/body/eval_jaxpr/ppermute | solution.py:24
  362.5 8.6 %collective-permute-start = (f32[5,256]{1,0:T(8,128)S(1)}, f32[5,256]{1,0:T(8,128)S(1)}, u32[]{:S(2)}, u32[]{:S(2)}) collective-permute-start(f32[5,256]{1,0:T(8,128)S(1)} %get-tuple-element.313), channel_id=1, source_target_pairs={{0,4},{4,8},{8,12},{12,16},{16,20},{20,24},{24,28},{28,32},{32,36}... | collective-permute-start | bytes 15368 | tf_op jit(solution)/shard_map/while/body/eval_jaxpr/ppermute | solution.py:24
  371.1 8.6 %collective-permute-start = (f32[5,256]{1,0:T(8,128)S(1)}, f32[5,256]{1,0:T(8,128)S(1)}, u32[]{:S(2)}, u32[]{:S(2)}) collective-permute-start(f32[5,256]{1,0:T(8,128)S(1)} %get-tuple-element.313), channel_id=1, source_target_pairs={{0,4},{4,8},{8,12},{12,16},{16,20},{20,24},{24,28},{28,32},{32,36}... | collective-permute-start | bytes 15368 | tf_op jit(solution)/shard_map/while/body/eval_jaxpr/ppermute | solution.py:24
  379.7 8.6 %collective-permute-start = (f32[5,256]{1,0:T(8,128)S(1)}, f32[5,256]{1,0:T(8,128)S(1)}, u32[]{:S(2)}, u32[]{:S(2)}) collective-permute-start(f32[5,256]{1,0:T(8,128)S(1)} %get-tuple-element.313), channel_id=1, source_target_pairs={{0,4},{4,8},{8,12},{12,16},{16,20},{20,24},{24,28},{28,32},{32,36}... | collective-permute-start | bytes 15368 | tf_op jit(solution)/shard_map/while/body/eval_jaxpr/ppermute | solution.py:24
  388.3 8.6 %collective-permute-start = (f32[5,256]{1,0:T(8,128)S(1)}, f32[5,256]{1,0:T(8,128)S(1)}, u32[]{:S(2)}, u32[]{:S(2)}) collective-permute-start(f32[5,256]{1,0:T(8,128)S(1)} %get-tuple-element.313), channel_id=1, source_target_pairs={{0,4},{4,8},{8,12},{12,16},{16,20},{20,24},{24,28},{28,32},{32,36}... | collective-permute-start | bytes 15368 | tf_op jit(solution)/shard_map/while/body/eval_jaxpr/ppermute | solution.py:24
  396.9 8.6 %collective-permute-start = (f32[5,256]{1,0:T(8,128)S(1)}, f32[5,256]{1,0:T(8,128)S(1)}, u32[]{:S(2)}, u32[]{:S(2)}) collective-permute-start(f32[5,256]{1,0:T(8,128)S(1)} %get-tuple-element.313), channel_id=1, source_target_pairs={{0,4},{4,8},{8,12},{12,16},{16,20},{20,24},{24,28},{28,32},{32,36}... | collective-permute-start | bytes 15368 | tf_op jit(solution)/shard_map/while/body/eval_jaxpr/ppermute | solution.py:24
  405.5 8.6 %collective-permute-start = (f32[5,256]{1,0:T(8,128)S(1)}, f32[5,256]{1,0:T(8,128)S(1)}, u32[]{:S(2)}, u32[]{:S(2)}) collective-permute-start(f32[5,256]{1,0:T(8,128)S(1)} %get-tuple-element.313), channel_id=1, source_target_pairs={{0,4},{4,8},{8,12},{12,16},{16,20},{20,24},{24,28},{28,32},{32,36}... | collective-permute-start | bytes 15368 | tf_op jit(solution)/shard_map/while/body/eval_jaxpr/ppermute | solution.py:24
  422.7 8.6 %collective-permute-start = (f32[5,256]{1,0:T(8,128)S(1)}, f32[5,256]{1,0:T(8,128)S(1)}, u32[]{:S(2)}, u32[]{:S(2)}) collective-permute-start(f32[5,256]{1,0:T(8,128)S(1)} %get-tuple-element.313), channel_id=1, source_target_pairs={{0,4},{4,8},{8,12},{12,16},{16,20},{20,24},{24,28},{28,32},{32,36}... | collective-permute-start | bytes 15368 | tf_op jit(solution)/shard_map/while/body/eval_jaxpr/ppermute | solution.py:24
  431.3 8.6 %collective-permute-start = (f32[5,256]{1,0:T(8,128)S(1)}, f32[5,256]{1,0:T(8,128)S(1)}, u32[]{:S(2)}, u32[]{:S(2)}) collective-permute-start(f32[5,256]{1,0:T(8,128)S(1)} %get-tuple-element.313), channel_id=1, source_target_pairs={{0,4},{4,8},{8,12},{12,16},{16,20},{20,24},{24,28},{28,32},{32,36}... | collective-permute-start | bytes 15368 | tf_op jit(solution)/shard_map/while/body/eval_jaxpr/ppermute | solution.py:24
  439.9 8.6 %collective-permute-start = (f32[5,256]{1,0:T(8,128)S(1)}, f32[5,256]{1,0:T(8,128)S(1)}, u32[]{:S(2)}, u32[]{:S(2)}) collective-permute-start(f32[5,256]{1,0:T(8,128)S(1)} %get-tuple-element.313), channel_id=1, source_target_pairs={{0,4},{4,8},{8,12},{12,16},{16,20},{20,24},{24,28},{28,32},{32,36}... | collective-permute-start | bytes 15368 | tf_op jit(solution)/shard_map/while/body/eval_jaxpr/ppermute | solution.py:24
  448.5 8.6 %collective-permute-start = (f32[5,256]{1,0:T(8,128)S(1)}, f32[5,256]{1,0:T(8,128)S(1)}, u32[]{:S(2)}, u32[]{:S(2)}) collective-permute-start(f32[5,256]{1,0:T(8,128)S(1)} %get-tuple-element.313), channel_id=1, source_target_pairs={{0,4},{4,8},{8,12},{12,16},{16,20},{20,24},{24,28},{28,32},{32,36}... | collective-permute-start | bytes 15368 | tf_op jit(solution)/shard_map/while/body/eval_jaxpr/ppermute | solution.py:24
  457.1 8.6 %collective-permute-start = (f32[5,256]{1,0:T(8,128)S(1)}, f32[5,256]{1,0:T(8,128)S(1)}, u32[]{:S(2)}, u32[]{:S(2)}) collective-permute-start(f32[5,256]{1,0:T(8,128)S(1)} %get-tuple-element.313), channel_id=1, source_target_pairs={{0,4},{4,8},{8,12},{12,16},{16,20},{20,24},{24,28},{28,32},{32,36}... | collective-permute-start | bytes 15368 | tf_op jit(solution)/shard_map/while/body/eval_jaxpr/ppermute | solution.py:24
  465.7 8.6 %collective-permute-start = (f32[5,256]{1,0:T(8,128)S(1)}, f32[5,256]{1,0:T(8,128)S(1)}, u32[]{:S(2)}, u32[]{:S(2)}) collective-permute-start(f32[5,256]{1,0:T(8,128)S(1)} %get-tuple-element.313), channel_id=1, source_target_pairs={{0,4},{4,8},{8,12},{12,16},{16,20},{20,24},{24,28},{28,32},{32,36}... | collective-permute-start | bytes 15368 | tf_op jit(solution)/shard_map/while/body/eval_jaxpr/ppermute | solution.py:24
  474.3 8.6 %collective-permute-start = (f32[5,256]{1,0:T(8,128)S(1)}, f32[5,256]{1,0:T(8,128)S(1)}, u32[]{:S(2)}, u32[]{:S(2)}) collective-permute-start(f32[5,256]{1,0:T(8,128)S(1)} %get-tuple-element.313), channel_id=1, source_target_pairs={{0,4},{4,8},{8,12},{12,16},{16,20},{20,24},{24,28},{28,32},{32,36}... | collective-permute-start | bytes 15368 | tf_op jit(solution)/shard_map/while/body/eval_jaxpr/ppermute | solution.py:24
  482.9 8.6 %collective-permute-start = (f32[5,256]{1,0:T(8,128)S(1)}, f32[5,256]{1,0:T(8,128)S(1)}, u32[]{:S(2)}, u32[]{:S(2)}) collective-permute-start(f32[5,256]{1,0:T(8,128)S(1)} %get-tuple-element.313), channel_id=1, source_target_pairs={{0,4},{4,8},{8,12},{12,16},{16,20},{20,24},{24,28},{28,32},{32,36}... | collective-permute-start | bytes 15368 | tf_op jit(solution)/shard_map/while/body/eval_jaxpr/ppermute | solution.py:24
  500.1 8.6 %collective-permute-start = (f32[5,256]{1,0:T(8,128)S(1)}, f32[5,256]{1,0:T(8,128)S(1)}, u32[]{:S(2)}, u32[]{:S(2)}) collective-permute-start(f32[5,256]{1,0:T(8,128)S(1)} %get-tuple-element.313), channel_id=1, source_target_pairs={{0,4},{4,8},{8,12},{12,16},{16,20},{20,24},{24,28},{28,32},{32,36}... | collective-permute-start | bytes 15368 | tf_op jit(solution)/shard_map/while/body/eval_jaxpr/ppermute | solution.py:24
  508.7 8.6 %collective-permute-start = (f32[5,256]{1,0:T(8,128)S(1)}, f32[5,256]{1,0:T(8,128)S(1)}, u32[]{:S(2)}, u32[]{:S(2)}) collective-permute-start(f32[5,256]{1,0:T(8,128)S(1)} %get-tuple-element.313), channel_id=1, source_target_pairs={{0,4},{4,8},{8,12},{12,16},{16,20},{20,24},{24,28},{28,32},{32,36}... | collective-permute-start | bytes 15368 | tf_op jit(solution)/shard_map/while/body/eval_jaxpr/ppermute | solution.py:24
  517.3 8.6 %collective-permute-start = (f32[5,256]{1,0:T(8,128)S(1)}, f32[5,256]{1,0:T(8,128)S(1)}, u32[]{:S(2)}, u32[]{:S(2)}) collective-permute-start(f32[5,256]{1,0:T(8,128)S(1)} %get-tuple-element.313), channel_id=1, source_target_pairs={{0,4},{4,8},{8,12},{12,16},{16,20},{20,24},{24,28},{28,32},{32,36}... | collective-permute-start | bytes 15368 | tf_op jit(solution)/shard_map/while/body/eval_jaxpr/ppermute | solution.py:24
  525.9 8.6 %collective-permute-start = (f32[5,256]{1,0:T(8,128)S(1)}, f32[5,256]{1,0:T(8,128)S(1)}, u32[]{:S(2)}, u32[]{:S(2)}) collective-permute-start(f32[5,256]{1,0:T(8,128)S(1)} %get-tuple-element.313), channel_id=1, source_target_pairs={{0,4},{4,8},{8,12},{12,16},{16,20},{20,24},{24,28},{28,32},{32,36}... | collective-permute-start | bytes 15368 | tf_op jit(solution)/shard_map/while/body/eval_jaxpr/ppermute | solution.py:24
  534.5 8.6 %collective-permute-start = (f32[5,256]{1,0:T(8,128)S(1)}, f32[5,256]{1,0:T(8,128)S(1)}, u32[]{:S(2)}, u32[]{:S(2)}) collective-permute-start(f32[5,256]{1,0:T(8,128)S(1)} %get-tuple-element.313), channel_id=1, source_target_pairs={{0,4},{4,8},{8,12},{12,16},{16,20},{20,24},{24,28},{28,32},{32,36}... | collective-permute-start | bytes 15368 | tf_op jit(solution)/shard_map/while/body/eval_jaxpr/ppermute | solution.py:24
  543.1 8.6 %collective-permute-start = (f32[5,256]{1,0:T(8,128)S(1)}, f32[5,256]{1,0:T(8,128)S(1)}, u32[]{:S(2)}, u32[]{:S(2)}) collective-permute-start(f32[5,256]{1,0:T(8,128)S(1)} %get-tuple-element.313), channel_id=1, source_target_pairs={{0,4},{4,8},{8,12},{12,16},{16,20},{20,24},{24,28},{28,32},{32,36}... | collective-permute-start | bytes 15368 | tf_op jit(solution)/shard_map/while/body/eval_jaxpr/ppermute | solution.py:24
  551.7 8.6 %collective-permute-start = (f32[5,256]{1,0:T(8,128)S(1)}, f32[5,256]{1,0:T(8,128)S(1)}, u32[]{:S(2)}, u32[]{:S(2)}) collective-permute-start(f32[5,256]{1,0:T(8,128)S(1)} %get-tuple-element.313), channel_id=1, source_target_pairs={{0,4},{4,8},{8,12},{12,16},{16,20},{20,24},{24,28},{28,32},{32,36}... | collective-permute-start | bytes 15368 | tf_op jit(solution)/shard_map/while/body/eval_jaxpr/ppermute | solution.py:24
  560.3 8.6 %collective-permute-start = (f32[5,256]{1,0:T(8,128)S(1)}, f32[5,256]{1,0:T(8,128)S(1)}, u32[]{:S(2)}, u32[]{:S(2)}) collective-permute-start(f32[5,256]{1,0:T(8,128)S(1)} %get-tuple-element.313), channel_id=1, source_target_pairs={{0,4},{4,8},{8,12},{12,16},{16,20},{20,24},{24,28},{28,32},{32,36}... | collective-permute-start | bytes 15368 | tf_op jit(solution)/shard_map/while/body/eval_jaxpr/ppermute | solution.py:24
  568.9 8.6 %collective-permute-start = (f32[5,256]{1,0:T(8,128)S(1)}, f32[5,256]{1,0:T(8,128)S(1)}, u32[]{:S(2)}, u32[]{:S(2)}) collective-permute-start(f32[5,256]{1,0:T(8,128)S(1)} %get-tuple-element.313), channel_id=1, source_target_pairs={{0,4},{4,8},{8,12},{12,16},{16,20},{20,24},{24,28},{28,32},{32,36}... | collective-permute-start | bytes 15368 | tf_op jit(solution)/shard_map/while/body/eval_jaxpr/ppermute | solution.py:24
  586.1 8.6 %collective-permute-start = (f32[5,256]{1,0:T(8,128)S(1)}, f32[5,256]{1,0:T(8,128)S(1)}, u32[]{:S(2)}, u32[]{:S(2)}) collective-permute-start(f32[5,256]{1,0:T(8,128)S(1)} %get-tuple-element.313), channel_id=1, source_target_pairs={{0,4},{4,8},{8,12},{12,16},{16,20},{20,24},{24,28},{28,32},{32,36}... | collective-permute-start | bytes 15368 | tf_op jit(solution)/shard_map/while/body/eval_jaxpr/ppermute | solution.py:24
  594.7 8.6 %collective-permute-start = (f32[5,256]{1,0:T(8,128)S(1)}, f32[5,256]{1,0:T(8,128)S(1)}, u32[]{:S(2)}, u32[]{:S(2)}) collective-permute-start(f32[5,256]{1,0:T(8,128)S(1)} %get-tuple-element.313), channel_id=1, source_target_pairs={{0,4},{4,8},{8,12},{12,16},{16,20},{20,24},{24,28},{28,32},{32,36}... | collective-permute-start | bytes 15368 | tf_op jit(solution)/shard_map/while/body/eval_jaxpr/ppermute | solution.py:24
  603.3 8.6 %collective-permute-start = (f32[5,256]{1,0:T(8,128)S(1)}, f32[5,256]{1,0:T(8,128)S(1)}, u32[]{:S(2)}, u32[]{:S(2)}) collective-permute-start(f32[5,256]{1,0:T(8,128)S(1)} %get-tuple-element.313), channel_id=1, source_target_pairs={{0,4},{4,8},{8,12},{12,16},{16,20},{20,24},{24,28},{28,32},{32,36}... | collective-permute-start | bytes 15368 | tf_op jit(solution)/shard_map/while/body/eval_jaxpr/ppermute | solution.py:24
  611.9 8.6 %collective-permute-start = (f32[5,256]{1,0:T(8,128)S(1)}, f32[5,256]{1,0:T(8,128)S(1)}, u32[]{:S(2)}, u32[]{:S(2)}) collective-permute-start(f32[5,256]{1,0:T(8,128)S(1)} %get-tuple-element.313), channel_id=1, source_target_pairs={{0,4},{4,8},{8,12},{12,16},{16,20},{20,24},{24,28},{28,32},{32,36}... | collective-permute-start | bytes 15368 | tf_op jit(solution)/shard_map/while/body/eval_jaxpr/ppermute | solution.py:24
  620.5 8.6 %collective-permute-start = (f32[5,256]{1,0:T(8,128)S(1)}, f32[5,256]{1,0:T(8,128)S(1)}, u32[]{:S(2)}, u32[]{:S(2)}) collective-permute-start(f32[5,256]{1,0:T(8,128)S(1)} %get-tuple-element.313), channel_id=1, source_target_pairs={{0,4},{4,8},{8,12},{12,16},{16,20},{20,24},{24,28},{28,32},{32,36}... | collective-permute-start | bytes 15368 | tf_op jit(solution)/shard_map/while/body/eval_jaxpr/ppermute | solution.py:24
  629.2 8.6 %collective-permute-start = (f32[5,256]{1,0:T(8,128)S(1)}, f32[5,256]{1,0:T(8,128)S(1)}, u32[]{:S(2)}, u32[]{:S(2)}) collective-permute-start(f32[5,256]{1,0:T(8,128)S(1)} %get-tuple-element.313), channel_id=1, source_target_pairs={{0,4},{4,8},{8,12},{12,16},{16,20},{20,24},{24,28},{28,32},{32,36}... | collective-permute-start | bytes 15368 | tf_op jit(solution)/shard_map/while/body/eval_jaxpr/ppermute | solution.py:24
  637.8 8.6 %collective-permute-start = (f32[5,256]{1,0:T(8,128)S(1)}, f32[5,256]{1,0:T(8,128)S(1)}, u32[]{:S(2)}, u32[]{:S(2)}) collective-permute-start(f32[5,256]{1,0:T(8,128)S(1)} %get-tuple-element.313), channel_id=1, source_target_pairs={{0,4},{4,8},{8,12},{12,16},{16,20},{20,24},{24,28},{28,32},{32,36}... | collective-permute-start | bytes 15368 | tf_op jit(solution)/shard_map/while/body/eval_jaxpr/ppermute | solution.py:24
  646.4 8.6 %collective-permute-start = (f32[5,256]{1,0:T(8,128)S(1)}, f32[5,256]{1,0:T(8,128)S(1)}, u32[]{:S(2)}, u32[]{:S(2)}) collective-permute-start(f32[5,256]{1,0:T(8,128)S(1)} %get-tuple-element.313), channel_id=1, source_target_pairs={{0,4},{4,8},{8,12},{12,16},{16,20},{20,24},{24,28},{28,32},{32,36}... | collective-permute-start | bytes 15368 | tf_op jit(solution)/shard_map/while/body/eval_jaxpr/ppermute | solution.py:24
  663.6 8.6 %collective-permute-start = (f32[5,256]{1,0:T(8,128)S(1)}, f32[5,256]{1,0:T(8,128)S(1)}, u32[]{:S(2)}, u32[]{:S(2)}) collective-permute-start(f32[5,256]{1,0:T(8,128)S(1)} %get-tuple-element.313), channel_id=1, source_target_pairs={{0,4},{4,8},{8,12},{12,16},{16,20},{20,24},{24,28},{28,32},{32,36}... | collective-permute-start | bytes 15368 | tf_op jit(solution)/shard_map/while/body/eval_jaxpr/ppermute | solution.py:24
  672.2 8.6 %collective-permute-start = (f32[5,256]{1,0:T(8,128)S(1)}, f32[5,256]{1,0:T(8,128)S(1)}, u32[]{:S(2)}, u32[]{:S(2)}) collective-permute-start(f32[5,256]{1,0:T(8,128)S(1)} %get-tuple-element.313), channel_id=1, source_target_pairs={{0,4},{4,8},{8,12},{12,16},{16,20},{20,24},{24,28},{28,32},{32,36}... | collective-permute-start | bytes 15368 | tf_op jit(solution)/shard_map/while/body/eval_jaxpr/ppermute | solution.py:24
  680.8 8.6 %collective-permute-start = (f32[5,256]{1,0:T(8,128)S(1)}, f32[5,256]{1,0:T(8,128)S(1)}, u32[]{:S(2)}, u32[]{:S(2)}) collective-permute-start(f32[5,256]{1,0:T(8,128)S(1)} %get-tuple-element.313), channel_id=1, source_target_pairs={{0,4},{4,8},{8,12},{12,16},{16,20},{20,24},{24,28},{28,32},{32,36}... | collective-permute-start | bytes 15368 | tf_op jit(solution)/shard_map/while/body/eval_jaxpr/ppermute | solution.py:24
  689.4 8.6 %collective-permute-start = (f32[5,256]{1,0:T(8,128)S(1)}, f32[5,256]{1,0:T(8,128)S(1)}, u32[]{:S(2)}, u32[]{:S(2)}) collective-permute-start(f32[5,256]{1,0:T(8,128)S(1)} %get-tuple-element.313), channel_id=1, source_target_pairs={{0,4},{4,8},{8,12},{12,16},{16,20},{20,24},{24,28},{28,32},{32,36}... | collective-permute-start | bytes 15368 | tf_op jit(solution)/shard_map/while/body/eval_jaxpr/ppermute | solution.py:24
  (231 other events, 1277.9 us)
where the time goes:
time: 827 us; the launch traced here: 819 us
  waiting for transfers between devices  430 us (52%)
  local copies, waits for them, and re-layouts  192 us (23%)
  starting transfers between devices  129 us (16%)
  other arithmetic  50.8 us (6%)
  matrix products  10.1 us (1%)
    ppermute x63, waiting for transfers between devices, passed_along(): lax.ppermute(value, axis, [(source, source + steps) for source in range(l...  417 us
    gather x96, local copies, waits for them, and re-layouts, reorient(): fetched[:, orientations[symmetry]]  123 us
    ppermute x63, starting transfers between devices, passed_along(): lax.ppermute(value, axis, [(source, source + steps) for source in range(l...  121 us
    gather x12, local copies, waits for them, and re-layouts, adjoint_step(): fetched = jnp.take(across, neighbors[k], axis=2)  25.9 us
    concatenate x12, local copies, waits for them, and re-layouts, adjoint_step(): across = jnp.concatenate([traces[k ^ 1], from_left, from_right], axis=2)  20.3 us
    select_n x18, other arithmetic, adjoint_step(): fetched = jnp.take(across, neighbors[k], axis=2)  18.8 us
  transfers between devices with their start and end apart: 68, of which 65 were waited for; matrix products, arithmetic and copies ran while one was open for 3% of the time, Pallas kernels for 0%

commit v1 on v0

v1 whole, which is shorter than its diff:
```python
import functools
import math

import jax
import jax.numpy as jnp
import ml_dtypes
import numpy as np
from jax import lax
from jax.experimental import pallas as pl
from jax.experimental.pallas import tpu as pltpu
from jax.sharding import PartitionSpec as P

MESH = pl.DeviceIdType.MESH
FIELDS = 5
NODES = 64
ROWS = FIELDS * NODES
ELEMS = 256
SURFACE = 128
STEP = 0.02
LIFT = 3.0
bf16 = jnp.bfloat16
f32 = jnp.float32


def tables():
    x = np.array([-1.0, -math.sqrt(0.2), math.sqrt(0.2), 1.0])
    bary = np.array([1.0 / np.prod([x[j] - x[k] for k in range(4) if k != j]) for j in range(4)])
    d1 = np.zeros((4, 4))
    for i in range(4):
        for j in range(4):
            if i != j:
                d1[i, j] = bary[j] / bary[i] / (x[i] - x[j])
        d1[i, i] = -d1[i].sum()
    eye = np.eye(4)
    derivs = [
        np.kron(np.kron(d1, eye), eye),
        np.kron(np.kron(eye, d1), eye),
        np.kron(np.kron(eye, eye), d1),
    ]
    w1 = np.array([1.0, 5.0, 5.0, 1.0]) / 6.0
    weights = (w1[:, None, None] * w1[None, :, None] * w1[None, None, :]).reshape(64) / 8.0
    n = np.arange(64)
    coords = [n // 16, n // 4 % 4, n % 4]
    blocks = []
    faces = np.zeros(64)
    for d in range(3):
        low, high = coords[d] == 0, coords[d] == 3
        faces += low.astype(float) + high.astype(float)
        blocks.append(STEP * (derivs[d].T + LIFT * np.diag(low.astype(float) - high.astype(float))))
    full = np.concatenate(blocks, axis=0)
    high_part = full.astype(ml_dtypes.bfloat16)
    low_part = (full - high_part.astype(np.float64)).astype(ml_dtypes.bfloat16)
    deriv = np.concatenate([high_part, high_part, low_part], axis=1)
    signs = [np.where(coords[d] == 0, -1.0, 1.0) for d in range(3)]
    own = 1.0 - STEP * LIFT * faces
    pattern = np.stack([weights, own] + signs).astype(np.float32)
    pattern = np.repeat(pattern.reshape(5 * 64, 1), 128, axis=1)
    return deriv, pattern


def face_node(k, p, q):
    if k < 2:
        return 48 * (k & 1) + 4 * p + q
    if k < 4:
        return 16 * p + 12 * (k & 1) + q
    return 16 * p + 4 * q + 3 * (k & 1)


def split(value):
    high = value.astype(bf16)
    low = (value - high.astype(f32)).astype(bf16)
    return jnp.concatenate([high, low], axis=0)


def gathered(both, chosen):
    out = jnp.dot(both, chosen, preferred_element_type=f32)
    half = out.shape[0] // 2
    return out[:half] + out[half:]


def one_hot(index_row, start, count):
    rows = lax.broadcasted_iota(jnp.int32, (count, index_row.shape[1]), 0) + start
    return jnp.where(rows == index_row, 1.0, 0.0).astype(bf16)


def wide(ref, *index):
    return jnp.concatenate([ref[(half, *index, slice(None))] for half in range(2)], axis=1)


def store_wide(ref, index, value):
    for half in range(2):
        ref[half, index, :] = value[:, 128 * half : 128 * half + 128]


def matvec(block, vector):
    total = wide(block, pl.ds(0, 5, stride=5)) * vector[0:1, :]
    for g in range(1, 5):
        total = total + wide(block, pl.ds(g, 5, stride=5)) * vector[g : g + 1, :]
    return total


def kernel(
    windows, parts, near, far,
    state_hbm, forcing_hbm, jac_hbm, coarse_hbm, neigh_hbm, orient_hbm, inter_hbm, deriv_hbm, pat_hbm,
    out_hbm,
    state, forcing, jac, coarse, neigh, orient, inter, deriv, pat,
    hot, hot_left, hot_right, hot_inter,
    fetched, lifted, terms, middle, start, shifted,
    halo_out, halo_in,
    blocks, products, ends, ends_next, coarse_out, coarse_in, window_out, window_in, result,
    in_sem, out_sem, halo_sem, block_sem, product_sem, end_sem, coarse_sem, window_sem, bulk_sem,
):
    tm = lax.axis_index("tm")
    space = lax.axis_index("space")

    def at_tm(distance):
        return {"tm": lax.rem(tm + (distance + windows), windows)}

    def at_space(distance):
        return {"space": lax.rem(space + (distance + parts), parts)}

    def send(src, dst, sems, index, target):
        copy = pltpu.make_async_remote_copy(
            src_ref=src, dst_ref=dst, send_sem=sems.at[0, index], recv_sem=sems.at[1, index],
            device_id=target, device_id_type=MESH,
        )
        copy.start()
        return copy

    loads = []
    for number, (src, dst) in enumerate([
        (inter_hbm, inter), (state_hbm, state), (neigh_hbm, neigh), (coarse_hbm, coarse),
        (orient_hbm, orient), (deriv_hbm, deriv), (pat_hbm, pat), (jac_hbm, jac), (forcing_hbm, forcing),
    ]):
        if dst is state:
            pair = [(src.at[:, 128 * half : 128 * half + 128], dst.at[half], 9 * half + number) for half in range(2)]
        else:
            pair = [(src, dst, number)]
        loads.append([pltpu.make_async_copy(a, b, in_sem.at[c]) for a, b, c in pair])
        for load in loads[-1]:
            load.start()

    def arrive(number):
        for load in loads[number]:
            load.wait()

    sources = sorted(set(range(1, near + 1)) | {near * m for m in range(1, far)} | {windows - 1})
    barrier = pltpu.get_barrier_semaphore()
    for distance in (1, -1):
        pl.semaphore_signal(barrier, inc=1, device_id=at_space(distance), device_id_type=MESH)
    for distance in sources:
        pl.semaphore_signal(barrier, inc=1, device_id=at_tm(-distance), device_id_type=MESH)

    lifted[...] = jnp.zeros_like(lifted)
    arrive(0)
    for side in range(2):
        hot_inter[side] = one_hot(inter[side : side + 1, :], 0, ELEMS)
    arrive(1)

    def trace_x(values, low):
        return jnp.concatenate([wide(values, slice(64 * f + low, 64 * f + low + 16)) for f in range(FIELDS)], axis=0)

    def halo_start(turn, values):
        right = split(trace_x(values, 48))
        left = split(trace_x(values, 0))
        halo_out[turn, 0] = gathered(right, hot_inter[1])
        halo_out[turn, 1] = gathered(left, hot_inter[0])
        return right, left

    def halo_send(turn):
        return [
            send(halo_out.at[turn, 0], halo_in.at[turn, 0], halo_sem, 2 * turn, at_space(1)),
            send(halo_out.at[turn, 1], halo_in.at[turn, 1], halo_sem, 2 * turn + 1, at_space(-1)),
        ]

    def local_part(values, right, left):
        store_wide(fetched, pl.ds(0, 80), gathered(right, hot[0]))
        store_wide(fetched, pl.ds(160, 80), gathered(left, hot[1]))
        for k in (2, 3):
            low = 8 if k == 2 else 0
            starts = [64 * f + 16 * a + low for f in range(FIELDS) for a in range(4)]
            rows = [wide(values, slice(first, first + 8)) for first in starts]
            store_wide(fetched, pl.ds(160 * k, 160), gathered(split(jnp.concatenate(rows, axis=0)), hot[k]))
        for k in (4, 5):
            low = 3 if k == 4 else 0
            rows = wide(values, pl.ds(low, 80, stride=4))
            store_wide(fetched, pl.ds(160 * k, 80), gathered(split(rows), hot[k]))
        for h in range(FIELDS):
            both = split(wide(values, slice(64 * h, 64 * h + 64)))
            stacked = jnp.concatenate([both, both[:64]], axis=0)
            terms[192 * h : 192 * h + 192, :] = jnp.dot(deriv[...], stacked, preferred_element_type=f32)

    def align(k):
        for half in range(2):
            code = orient[k : k + 1, 128 * half : 128 * half + 128]
            swap, flip_p, flip_q = [jnp.broadcast_to(code & bit, (FIELDS, 128)) != 0 for bit in (4, 2, 1)]
            grid = [[None] * 4 for _ in range(4)]
            for p in range(4):
                for q in range(4):
                    if k in (2, 3):
                        first, stride = 8 * p + (4 if k == 2 else 0) + q, 32
                    else:
                        first, stride = 4 * p + q, 16
                    grid[p][q] = fetched[half, pl.ds(160 * k + first, FIELDS, stride=stride), :]
            grid = [[grid[p][q] if p == q else jnp.where(swap, grid[q][p], grid[p][q]) for q in range(4)] for p in range(4)]
            grid = [[jnp.where(flip_p, grid[3 - p][q], grid[p][q]) for q in range(4)] for p in range(4)]
            grid = [[jnp.where(flip_q, grid[p][3 - q], grid[p][q]) for q in range(4)] for p in range(4)]
            for p in range(4):
                for q in range(4):
                    row = (k // 2 * 64 + face_node(k, p, q)) * 8
                    lifted[half, row : row + FIELDS, :] = (STEP * LIFT) * grid[p][q]

    def halo_part(turn):
        for side, chosen in enumerate((hot_left, hot_right)):
            rows = pl.ds(160 * side, 80)
            total = wide(fetched, rows) + gathered(split(halo_in[turn, side]), chosen[...])
            store_wide(fetched, rows, total)

    def mix(values, source, target):
        for group in range(2):
            low = 32 * group
            for half in range(2):
                lanes = slice(128 * half, 128 * half + 128)
                own = pat[64 + low : 96 + low, :]
                totals = [
                    own * values[half, 64 * f + low : 64 * f + low + 32, :]
                    + forcing[source, 64 * f + low : 64 * f + low + 32, lanes].astype(f32)
                    for f in range(FIELDS)
                ]
                for d in range(3):
                    sign = pat[128 + 64 * d + low : 160 + 64 * d + low, :]
                    for h in range(FIELDS):
                        face = lifted[half, pl.ds((64 * d + low) * 8 + h, 32, stride=8), :]
                        base = 192 * h + 64 * d + low
                        term = terms[base : base + 32, lanes] + sign * face
                        totals[h] = totals[h] + face
                        for f in range(FIELDS):
                            totals[f] = totals[f] + jac[5 * d + h, f : f + 1, lanes] * term
                for f in range(FIELDS):
                    target[half, 64 * f + low : 64 * f + low + 32, :] = totals[f]

    def node_sum(values):
        sums = []
        for f in range(FIELDS):
            halves = [
                jnp.sum(pat[0:64, :] * values[half, 64 * f : 64 * f + 64, :], axis=0, keepdims=True)
                for half in range(2)
            ]
            sums.append(jnp.concatenate(halves, axis=1))
        return jnp.concatenate(sums, axis=0)

    copies = []
    right, left = halo_start(0, state)
    pl.semaphore_wait(barrier, len(sources) + 2)
    halo = halo_send(0)
    arrive(3)
    keep = jnp.where(tm == 0, 0.0, 1.0)
    for f in range(FIELDS):
        store_wide(blocks.at[0], pl.ds(5 * f, 5), coarse[f] * keep)
    for m in range(1, near):
        copies.append(send(blocks.at[0], blocks.at[m], block_sem, m, at_tm(m)))
    arrive(6)
    ends[...] = node_sum(state)
    end_copy = send(ends, ends_next, end_sem, 0, at_tm(-1))
    arrive(2)
    for k in range(6):
        hot[k] = one_hot(neigh[k : k + 1, :], 0, ELEMS)
    hot_left[...] = one_hot(neigh[0:1, :], ELEMS, SURFACE)
    hot_right[...] = one_hot(neigh[1:2, :], ELEMS + SURFACE, SURFACE)
    arrive(5)
    local_part(state, right, left)
    arrive(4)
    for k in range(2, 6):
        align(k)
    for copy in halo:
        copy.wait()
    halo_part(0)
    align(0)
    align(1)
    arrive(7)
    arrive(8)
    mix(state, 1, middle)

    right, left = halo_start(1, middle)
    halo = halo_send(1)
    local_part(middle, right, left)
    for k in range(2, 6):
        align(k)
    for copy in copies:
        copy.wait()
    columns = [wide(blocks.at[near - 1], pl.ds(g, 5, stride=5)) for g in range(5)]
    for m in range(near - 2, -1, -1):
        columns = [matvec(blocks.at[m], column) for column in columns]
    for g in range(5):
        store_wide(products.at[0], pl.ds(g, 5, stride=5), columns[g])
    copies = [send(products.at[0], products.at[m], product_sem, m, at_tm(near * m)) for m in range(1, far - 1)]
    for copy in halo:
        copy.wait()
    halo_part(1)
    align(0)
    align(1)
    mix(middle, 0, start)

    end_copy.wait()
    coarse_out[...] = node_sum(start) - ends_next[...]
    rounds = [send(coarse_out, coarse_in.at[m], coarse_sem, m, at_tm(m + 1)) for m in range(near)]
    bulk = [
        send(start.at[:, pl.ds(64 * f, 64)], shifted.at[:, pl.ds(64 * f, 64)], bulk_sem, f, at_tm(1))
        for f in range(FIELDS)
    ]
    for copy in rounds:
        copy.wait()
    vector = coarse_in[near - 1]
    for m in range(near - 2, -1, -1):
        vector = coarse_in[m] + matvec(blocks.at[m], vector)
    window_out[...] = vector
    rounds = [send(window_out, window_in.at[m], window_sem, m, at_tm(near * m)) for m in range(1, far)]
    for copy in copies:
        copy.wait()
    for copy in rounds:
        copy.wait()
    vector = window_in[far - 1]
    for m in range(far - 2, 0, -1):
        vector = window_in[m] + matvec(products.at[m], vector)
    vector = window_out[...] + matvec(products.at[0], vector)
    outs = []
    for f in range(FIELDS):
        bulk[f].wait()
        rows = pl.ds(64 * f, 64)
        result[rows, :] = wide(shifted, rows) + vector[f : f + 1, :]
        copy = pltpu.make_async_copy(result.at[rows], out_hbm.at[rows], out_sem.at[f])
        copy.start()
        outs.append(copy)
    for copy in outs:
        copy.wait()


def solution(mesh):
    windows, parts = mesh.shape["tm"], mesh.shape["space"]
    near = 2 ** ((windows.bit_length() - 1) // 2)
    far = windows // near
    deriv, pattern = tables()
    dma = pltpu.SemaphoreType.DMA

    def per_device(end_state, forcing, jacobians, coarse_blocks, neighbors, orientation, interfaces):
        operands = (
            end_state.reshape(ROWS, ELEMS),
            forcing.reshape(2, ROWS, ELEMS),
            jacobians.reshape(15, 5, ELEMS),
            coarse_blocks.reshape(5, 5, ELEMS),
            neighbors,
            orientation,
            interfaces,
            jnp.asarray(deriv, bf16),
            jnp.asarray(pattern, f32),
        )
        out = pl.pallas_call(
            functools.partial(kernel, windows, parts, near, far),
            out_shape=jax.ShapeDtypeStruct((ROWS, ELEMS), f32),
            in_specs=[pl.BlockSpec(memory_space=pl.ANY)] * len(operands),
            out_specs=pl.BlockSpec(memory_space=pl.ANY),
            scratch_shapes=[pltpu.VMEM((2, ROWS, 128), f32)]
            + [pltpu.VMEM(x.shape, x.dtype) for x in operands[1:]]
            + [
                pltpu.VMEM((6, ELEMS, ELEMS), bf16),
                pltpu.VMEM((SURFACE, ELEMS), bf16),
                pltpu.VMEM((SURFACE, ELEMS), bf16),
                pltpu.VMEM((2, ELEMS, SURFACE), bf16),
                pltpu.VMEM((2, 6 * 160, 128), f32),
                pltpu.VMEM((2, 3 * 64 * 8, 128), f32),
                pltpu.VMEM((15 * 64, ELEMS), f32),
                pltpu.VMEM((2, ROWS, 128), f32),
                pltpu.VMEM((2, ROWS, 128), f32),
                pltpu.VMEM((2, ROWS, 128), f32),
                pltpu.VMEM((2, 2, 80, SURFACE), f32),
                pltpu.VMEM((2, 2, 80, SURFACE), f32),
                pltpu.VMEM((near, 2, 25, 128), f32),
                pltpu.VMEM((max(far - 1, 1), 2, 25, 128), f32),
                pltpu.VMEM((5, ELEMS), f32),
                pltpu.VMEM((5, ELEMS), f32),
                pltpu.VMEM((5, ELEMS), f32),
                pltpu.VMEM((near, 5, ELEMS), f32),
                pltpu.VMEM((5, ELEMS), f32),
                pltpu.VMEM((far, 5, ELEMS), f32),
                pltpu.VMEM((ROWS, ELEMS), f32),
                dma((18,)),
                dma((5,)),
                dma((2, 4)),
                dma((2, near)),
                dma((2, far)),
                dma((2, 1)),
                dma((2, near)),
                dma((2, far)),
                dma((2, 5)),
            ],
            compiler_params=pltpu.CompilerParams(
                collective_id=0, has_side_effects=True, vmem_limit_bytes=32 * 2**20
            ),
        )(*operands)
        return out.reshape(1, FIELDS, NODES, ELEMS)

    in_specs = (
        P("tm", None, None, "space"),
        P("tm", None, None, None, "space"),
        P("tm", None, None, None, "space"),
        P("tm", None, None, "space"),
        P(None, "space"),
        P(None, "space"),
        P(None, "space"),
    )
    out_specs = P("tm", None, None, "space")
    return jax.shard_map(per_device, mesh=mesh, in_specs=in_specs, out_specs=out_specs, check_vma=False)
```

time: 827 us -> 44.8 us (0.05)
  the two profiles are of different devices: /device:TPU:24 before, /device:TPU:6 now
where the time goes in v1:
time: 44.8 us; the launch traced here: 44.6 us
  Pallas kernels  38.8 us (87%)
  local copies, waits for them, and re-layouts  5.74 us (13%)
    pallas_call x1, Pallas kernels, per_device(): pl.pallas_call(functools.partial(kernel, windows, parts, near, far), out_...  38.8 us
    unnamed x17, local copies, waits for them, and re-layouts  5.74 us

profile of v1, /device:TPU:6, one launch (start us, length us, event | category | flops | bytes accessed | tf_op | source)
XLA Modules:
  0.0 44.6 jit_solution(7492758754774096257)
XLA Ops:
  0.0 0.0 copy-start.2
  0.0 0.8 %copy.16 = f32[1,5,5,256]{3,2,0,1:T(8,128)S(1)} copy(f32[1,5,5,256]{3,0,2,1:T(1,128)} %param.12) | data formatting | bytes 51200
  0.8 0.0 copy-start.3
  0.8 0.0 copy-start.4
  0.8 0.9 %copy.13 = f32[1,3,5,5,256]{4,3,0,2,1:T(8,128)S(1)} copy(f32[1,3,5,5,256]{4,0,3,2,1:T(1,128)} %param.11) | data formatting | bytes 153600
  1.7 0.0 copy-start.6
  1.7 0.0 copy-done.2
  1.8 0.0 copy-done.3
  1.8 0.0 copy-done.4
  1.8 0.6 %copy-done.6 = s32[2,128]{1,0:T(2,128)S(1)} copy-done((s32[2,128]{1,0:T(2,128)S(1)}, s32[2,128]{1,0:T(2,128)}, u32[]{:S(2)}) %copy-start.6) | copy-done | bytes 1048
  2.4 0.0 copy-start
  2.4 1.0 %copy-done = f32[1,5,64,256]{3,2,1,0:T(8,128)S(1)} copy-done((f32[1,5,64,256]{3,2,1,0:T(8,128)S(1)}, f32[1,5,64,256]{3,2,1,0:T(8,128)}, u32[]{:S(2)}) %copy-start) | copy-done | bytes 327704
  3.4 0.0 copy-start.1
  3.4 1.0 %copy-done.1 = bf16[1,2,5,64,256]{4,3,2,1,0:T(8,128)(2,1)S(1)} copy-done((bf16[1,2,5,64,256]{4,3,2,1,0:T(8,128)(2,1)S(1)}, bf16[1,2,5,64,256]{4,3,2,1,0:T(8,128)(2,1)}, u32[]{:S(2)}) %copy-start.1) | copy-done | bytes 327704
  4.4 0.0 copy-start.5
  4.4 0.7 %copy-done.5 = s32[6,256]{1,0:T(8,128)S(1)} copy-done((s32[6,256]{1,0:T(8,128)S(1)}, s32[6,256]{1,0:T(8,128)}, u32[]{:S(2)}) %copy-start.5) | copy-done | bytes 6168
  5.1 38.8 %shard_map.91 = f32[320,256]{1,0:T(8,128)S(1)} custom-call(f32[320,256]{1,0:T(8,128)S(1)} %bitcast.9, bf16[2,320,256]{2,1,0:T(8,128)(2,1)S(1)} %bitcast.10, f32[15,5,256]{2,1,0:T(8,128)S(1)} %bitcast.8, f32[5,5,256]{2,1,0:T(8,128)S(1)} %bitcast.11, s32[6,256]{1,0:T(8,128)S(1)} %copy-done.4, s32[6,256]{1,0:T(8,128)S(1)} %copy-done.5, s32[2,128]{1,0:T(2,128)S(1)} %copy-done.6, ...), custom_call_target="tpu_custom_call" | custom-call | tf_op jit(solution)/shard_map/pallas_call | solution.py:357
  43.8 0.7 %copy.18 = f32[1,5,64,256]{3,2,1,0:T(8,128)} copy(f32[1,5,64,256]{3,2,1,0:T(8,128)S(1)} %bitcast.7) | data formatting | bytes 655360
Async XLA Ops:
  0.0 1.7 %copy-start.2 = (f32[320,128]{1,0:T(8,128)S(1)}, f32[320,128]{1,0:T(8,128)}, u32[]{:S(2)}) copy-start(f32[320,128]{1,0:T(8,128)} %constant.5.clone.pat_hbm) | copy-start | bytes 491524
  0.8 1.0 %copy-start.3 = (bf16[192,192]{1,0:T(8,128)(2,1)S(1)}, bf16[192,192]{1,0:T(8,128)(2,1)}, u32[]{:S(2)}) copy-start(bf16[192,192]{1,0:T(8,128)(2,1)} %constant.4.clone.deriv_hbm) | copy-start | bytes 221188
  0.8 1.0 %copy-start.4 = (s32[6,256]{1,0:T(8,128)S(1)}, s32[6,256]{1,0:T(8,128)}, u32[]{:S(2)}) copy-start(s32[6,256]{1,0:T(8,128)} %neigh_hbm.1) | copy-start | bytes 18436
  1.7 0.7 %copy-start.6 = (s32[2,128]{1,0:T(2,128)S(1)}, s32[2,128]{1,0:T(2,128)}, u32[]{:S(2)}) copy-start(s32[2,128]{1,0:T(2,128)} %inter_hbm.1) | copy-start | bytes 3076
  2.4 1.0 %copy-start = (f32[1,5,64,256]{3,2,1,0:T(8,128)S(1)}, f32[1,5,64,256]{3,2,1,0:T(8,128)}, u32[]{:S(2)}) copy-start(f32[1,5,64,256]{3,2,1,0:T(8,128)} %param.9) | copy-start | bytes 983044
  3.4 1.0 %copy-start.1 = (bf16[1,2,5,64,256]{4,3,2,1,0:T(8,128)(2,1)S(1)}, bf16[1,2,5,64,256]{4,3,2,1,0:T(8,128)(2,1)}, u32[]{:S(2)}) copy-start(bf16[1,2,5,64,256]{4,3,2,1,0:T(8,128)(2,1)} %param.10) | copy-start | bytes 983044
  4.4 0.7 %copy-start.5 = (s32[6,256]{1,0:T(8,128)S(1)}, s32[6,256]{1,0:T(8,128)}, u32[]{:S(2)}) copy-start(s32[6,256]{1,0:T(8,128)} %orient_hbm.1) | copy-start | bytes 18436

commit v2 on v1

--- a/solution.py
+++ b/solution.py
@@ -18,6 +18,7 @@
 SURFACE = 128
 STEP = 0.02
 LIFT = 3.0
+EARLY = 2
 bf16 = jnp.bfloat16
 f32 = jnp.float32
 
@@ -92,23 +93,27 @@
         ref[half, index, :] = value[:, 128 * half : 128 * half + 128]
 
 
+def column(block, g):
+    return jnp.concatenate([block[pl.ds(2 * g + half, 5, stride=10), :] for half in range(2)], axis=1)
+
+
 def matvec(block, vector):
-    total = wide(block, pl.ds(0, 5, stride=5)) * vector[0:1, :]
+    total = column(block, 0) * vector[0:1, :]
     for g in range(1, 5):
-        total = total + wide(block, pl.ds(g, 5, stride=5)) * vector[g : g + 1, :]
+        total = total + column(block, g) * vector[g : g + 1, :]
     return total
 
 
 def kernel(
     windows, parts, near, far,
     state_hbm, forcing_hbm, jac_hbm, coarse_hbm, neigh_hbm, orient_hbm, inter_hbm, deriv_hbm, pat_hbm,
-    out_hbm,
+    shifted, correction,
     state, forcing, jac, coarse, neigh, orient, inter, deriv, pat,
     hot, hot_left, hot_right, hot_inter,
-    fetched, lifted, terms, middle, start, shifted,
+    fetched, lifted, terms, middle, start,
     halo_out, halo_in,
-    blocks, products, ends, ends_next, coarse_out, coarse_in, window_out, window_in, result,
-    in_sem, out_sem, halo_sem, block_sem, product_sem, end_sem, coarse_sem, window_sem, bulk_sem,
+    blocks, products, ends, ends_next, coarse_out, coarse_in, window_out, window_in,
+    in_sem, halo_sem, block_sem, product_sem, end_sem, coarse_sem, window_sem, bulk_sem,
 ):
     tm = lax.axis_index("tm")
     space = lax.axis_index("space")
@@ -127,10 +132,14 @@
         copy.start()
         return copy
 
+    sources = sorted(set(range(1, near + 1)) | {near * m for m in range(1, far)} | {windows - 1})
+    barrier = pltpu.get_barrier_semaphore()
+    for distance in (1, -1):
+        pl.semaphore_signal(barrier, inc=1, device_id=at_space(distance), device_id_type=MESH)
     loads = []
     for number, (src, dst) in enumerate([
-        (inter_hbm, inter), (state_hbm, state), (neigh_hbm, neigh), (coarse_hbm, coarse),
-        (orient_hbm, orient), (deriv_hbm, deriv), (pat_hbm, pat), (jac_hbm, jac), (forcing_hbm, forcing),
+        (inter_hbm, inter), (state_hbm, state), (neigh_hbm, neigh), (coarse_hbm.at[:, 0, :], coarse),
+        (orient_hbm, orient), (deriv_hbm, deriv), (pat_hbm, pat), (jac_hbm.at[:, 0, :], jac), (forcing_hbm, forcing),
     ]):
         if dst is state:
             pair = [(src.at[:, 128 * half : 128 * half + 128], dst.at[half], 9 * half + number) for half in range(2)]
@@ -140,18 +149,13 @@
         for load in loads[-1]:
             load.start()
 
+    for distance in sources:
+        pl.semaphore_signal(barrier, inc=1, device_id=at_tm(-distance), device_id_type=MESH)
+
     def arrive(number):
         for load in loads[number]:
             load.wait()
 
-    sources = sorted(set(range(1, near + 1)) | {near * m for m in range(1, far)} | {windows - 1})
-    barrier = pltpu.get_barrier_semaphore()
-    for distance in (1, -1):
-        pl.semaphore_signal(barrier, inc=1, device_id=at_space(distance), device_id_type=MESH)
-    for distance in sources:
-        pl.semaphore_signal(barrier, inc=1, device_id=at_tm(-distance), device_id_type=MESH)
-
-    lifted[...] = jnp.zeros_like(lifted)
     arrive(0)
     for side in range(2):
         hot_inter[side] = one_hot(inter[side : side + 1, :], 0, ELEMS)
@@ -216,7 +220,13 @@
             total = wide(fetched, rows) + gathered(split(halo_in[turn, side]), chosen[...])
             store_wide(fetched, rows, total)
 
-    def mix(values, source, target):
+    def store_middle(row, half, value):
+        middle[half, row : row + 32, :] = value
+
+    def store_start(row, half, value):
+        start[row : row + 32, 128 * half : 128 * half + 128] = value
+
+    def mix(values, source, store):
         for group in range(2):
             low = 32 * group
             for half in range(2):
@@ -235,17 +245,14 @@
                         term = terms[base : base + 32, lanes] + sign * face
                         totals[h] = totals[h] + face
                         for f in range(FIELDS):
-                            totals[f] = totals[f] + jac[5 * d + h, f : f + 1, lanes] * term
+                            totals[f] = totals[f] + jac[10 * (5 * d + h) + 2 * f + half : 10 * (5 * d + h) + 2 * f + half + 1, :] * term
                 for f in range(FIELDS):
-                    target[half, 64 * f + low : 64 * f + low + 32, :] = totals[f]
-
-    def node_sum(values):
+                    store(64 * f + low, half, totals[f])
+
+    def node_sum(piece):
         sums = []
         for f in range(FIELDS):
-            halves = [
-                jnp.sum(pat[0:64, :] * values[half, 64 * f : 64 * f + 64, :], axis=0, keepdims=True)
-                for half in range(2)
-            ]
+            halves = [jnp.sum(pat[0:64, :] * piece(64 * f, half), axis=0, keepdims=True) for half in range(2)]
             sums.append(jnp.concatenate(halves, axis=1))
         return jnp.concatenate(sums, axis=0)
 
@@ -253,14 +260,14 @@
     right, left = halo_start(0, state)
     pl.semaphore_wait(barrier, len(sources) + 2)
     halo = halo_send(0)
+    lifted[...] = jnp.zeros_like(lifted)
     arrive(3)
     keep = jnp.where(tm == 0, 0.0, 1.0)
-    for f in range(FIELDS):
-        store_wide(blocks.at[0], pl.ds(5 * f, 5), coarse[f] * keep)
+    blocks[0] = coarse[...] * keep
     for m in range(1, near):
         copies.append(send(blocks.at[0], blocks.at[m], block_sem, m, at_tm(m)))
     arrive(6)
-    ends[...] = node_sum(state)
+    ends[...] = node_sum(lambda row, half: state[half, row : row + 64, :])
     end_copy = send(ends, ends_next, end_sem, 0, at_tm(-1))
     arrive(2)
     for k in range(6):
@@ -279,35 +286,38 @@
     align(1)
     arrive(7)
     arrive(8)
-    mix(state, 1, middle)
+    mix(state, 1, store_middle)
 
     right, left = halo_start(1, middle)
     halo = halo_send(1)
     local_part(middle, right, left)
     for k in range(2, 6):
         align(k)
-    for copy in copies:
-        copy.wait()
-    columns = [wide(blocks.at[near - 1], pl.ds(g, 5, stride=5)) for g in range(5)]
-    for m in range(near - 2, -1, -1):
-        columns = [matvec(blocks.at[m], column) for column in columns]
-    for g in range(5):
-        store_wide(products.at[0], pl.ds(g, 5, stride=5), columns[g])
-    copies = [send(products.at[0], products.at[m], product_sem, m, at_tm(near * m)) for m in range(1, far - 1)]
     for copy in halo:
         copy.wait()
     halo_part(1)
     align(0)
     align(1)
-    mix(middle, 0, start)
+    mix(middle, 0, store_start)
 
     end_copy.wait()
-    coarse_out[...] = node_sum(start) - ends_next[...]
+    coarse_out[...] = node_sum(lambda row, half: start[row : row + 64, 128 * half : 128 * half + 128]) - ends_next[...]
     rounds = [send(coarse_out, coarse_in.at[m], coarse_sem, m, at_tm(m + 1)) for m in range(near)]
-    bulk = [
-        send(start.at[:, pl.ds(64 * f, 64)], shifted.at[:, pl.ds(64 * f, 64)], bulk_sem, f, at_tm(1))
-        for f in range(FIELDS)
-    ]
+    def bulk_send(fields):
+        return [
+            send(start.at[pl.ds(64 * f, 64)], shifted.at[pl.ds(64 * f, 64)], bulk_sem, f, at_tm(1)) for f in fields
+        ]
+
+    bulk = bulk_send(range(EARLY))
+    for copy in copies:
+        copy.wait()
+    columns = [column(blocks.at[near - 1], g) for g in range(5)]
+    for m in range(near - 2, -1, -1):
+        columns = [matvec(blocks.at[m], vector) for vector in columns]
+    for g in range(5):
+        for half in range(2):
+            products[0, pl.ds(2 * g + half, 5, stride=10), :] = columns[g][:, 128 * half : 128 * half + 128]
+    copies = [send(products.at[0], products.at[m], product_sem, m, at_tm(near * m)) for m in range(1, far - 1)]
     for copy in rounds:
         copy.wait()
     vector = coarse_in[near - 1]
@@ -315,6 +325,7 @@
         vector = coarse_in[m] + matvec(blocks.at[m], vector)
     window_out[...] = vector
     rounds = [send(window_out, window_in.at[m], window_sem, m, at_tm(near * m)) for m in range(1, far)]
+    bulk += bulk_send(range(EARLY, FIELDS))
     for copy in copies:
         copy.wait()
     for copy in rounds:
@@ -322,16 +333,8 @@
     vector = window_in[far - 1]
     for m in range(far - 2, 0, -1):
         vector = window_in[m] + matvec(products.at[m], vector)
-    vector = window_out[...] + matvec(products.at[0], vector)
-    outs = []
-    for f in range(FIELDS):
-        bulk[f].wait()
-        rows = pl.ds(64 * f, 64)
-        result[rows, :] = wide(shifted, rows) + vector[f : f + 1, :]
-        copy = pltpu.make_async_copy(result.at[rows], out_hbm.at[rows], out_sem.at[f])
-        copy.start()
-        outs.append(copy)
-    for copy in outs:
+    correction[...] = window_out[...] + matvec(products.at[0], vector)
+    for copy in bulk:
         copy.wait()
 
 
@@ -346,21 +349,21 @@
         operands = (
             end_state.reshape(ROWS, ELEMS),
             forcing.reshape(2, ROWS, ELEMS),
-            jacobians.reshape(15, 5, ELEMS),
-            coarse_blocks.reshape(5, 5, ELEMS),
+            jacobians.reshape(150, 1, 128),
+            coarse_blocks.reshape(50, 1, 128),
             neighbors,
             orientation,
             interfaces,
             jnp.asarray(deriv, bf16),
             jnp.asarray(pattern, f32),
         )
-        out = pl.pallas_call(
+        shifted, correction = pl.pallas_call(
             functools.partial(kernel, windows, parts, near, far),
-            out_shape=jax.ShapeDtypeStruct((ROWS, ELEMS), f32),
+            out_shape=(jax.ShapeDtypeStruct((ROWS, ELEMS), f32), jax.ShapeDtypeStruct((FIELDS, ELEMS), f32)),
             in_specs=[pl.BlockSpec(memory_space=pl.ANY)] * len(operands),
-            out_specs=pl.BlockSpec(memory_space=pl.ANY),
+            out_specs=(pl.BlockSpec(memory_space=pl.ANY), pl.BlockSpec(memory_space=pltpu.VMEM)),
             scratch_shapes=[pltpu.VMEM((2, ROWS, 128), f32)]
-            + [pltpu.VMEM(x.shape, x.dtype) for x in operands[1:]]
+            + [pltpu.VMEM((x.shape[0], 128) if x.shape[1] == 1 else x.shape, x.dtype) for x in operands[1:]]
             + [
                 pltpu.VMEM((6, ELEMS, ELEMS), bf16),
                 pltpu.VMEM((SURFACE, ELEMS), bf16),
@@ -370,21 +373,18 @@
                 pltpu.VMEM((2, 3 * 64 * 8, 128), f32),
                 pltpu.VMEM((15 * 64, ELEMS), f32),
                 pltpu.VMEM((2, ROWS, 128), f32),
-                pltpu.VMEM((2, ROWS, 128), f32),
-                pltpu.VMEM((2, ROWS, 128), f32),
+                pltpu.VMEM((ROWS, ELEMS), f32),
                 pltpu.VMEM((2, 2, 80, SURFACE), f32),
                 pltpu.VMEM((2, 2, 80, SURFACE), f32),
-                pltpu.VMEM((near, 2, 25, 128), f32),
-                pltpu.VMEM((max(far - 1, 1), 2, 25, 128), f32),
+                pltpu.VMEM((near, 50, 128), f32),
+                pltpu.VMEM((max(far - 1, 1), 50, 128), f32),
                 pltpu.VMEM((5, ELEMS), f32),
                 pltpu.VMEM((5, ELEMS), f32),
                 pltpu.VMEM((5, ELEMS), f32),
                 pltpu.VMEM((near, 5, ELEMS), f32),
                 pltpu.VMEM((5, ELEMS), f32),
                 pltpu.VMEM((far, 5, ELEMS), f32),
-                pltpu.VMEM((ROWS, ELEMS), f32),
                 dma((18,)),
-                dma((5,)),
                 dma((2, 4)),
                 dma((2, near)),
                 dma((2, far)),
@@ -394,10 +394,10 @@
                 dma((2, 5)),
             ],
             compiler_params=pltpu.CompilerParams(
-                collective_id=0, has_side_effects=True, vmem_limit_bytes=32 * 2**20
+                collective_id=0, has_side_effects=True, vmem_limit_bytes=60 * 2**20
             ),
         )(*operands)
-        return out.reshape(1, FIELDS, NODES, ELEMS)
+        return shifted.reshape(1, FIELDS, NODES, ELEMS) + correction[None, :, None, :]
 
     in_specs = (
         P("tm", None, None, "space"),

time: 44.8 us -> 37.5 us (0.84)
  the two profiles are of different devices: /device:TPU:6 before, /device:TPU:1 now
where the time goes in v2:
time: 37.5 us; the launch traced here: 37.4 us
  Pallas kernels  35.7 us (95%)
  other arithmetic  1.73 us (5%)
    pallas_call x1, Pallas kernels, per_device(): pl.pallas_call(functools.partial(kernel, windows, parts, near, far), out_...  35.7 us
    add x1, other arithmetic, per_device(): shifted.reshape(1, FIELDS, NODES, ELEMS) + correction[None, :, None, :]  1.73 us

profile of v2, /device:TPU:1, one launch (start us, length us, event | category | flops | bytes accessed | tf_op | source)
XLA Modules:
  0.0 37.4 jit_solution(1832424164989506318)
XLA Ops:
  0.0 35.7 %shard_map.91 = (f32[320,256]{1,0:T(8,128)}, f32[5,256]{1,0:T(8,128)}) custom-call(f32[320,256]{1,0:T(8,128)} %bitcast.5, bf16[2,320,256]{2,1,0:T(8,128)(2,1)} %bitcast.6, f32[150,1,128]{2,1,0:T(1,128)} %bitcast.8, f32[50,1,128]{2,1,0:T(1,128)} %bitcast.9, s32[6,256]{1,0:T(8,128)} %neigh_hbm.1, s32[6,256]{1,0:T(8,128)} %orient_hbm.1, s32[2,128]{1,0:T(2,128)} %inter_hbm.1, ...), custom_call_target="tpu_custom_call" | custom-call | tf_op jit(solution)/shard_map/pallas_call | solution.py:360
  35.7 1.7 %broadcast_add_fusion = f32[1,5,64,256]{3,2,1,0:T(8,128)} fusion(f32[1,5,64,256]{3,2,1,0:T(8,128)} %bitcast.7, f32[5,256]{1,0:T(8,128)} %get-tuple-element.8), kind=kLoop, calls=%fused_computation | loop fusion | flops 81920 | bytes 660480 | tf_op jit(solution)/shard_map/add | solution.py:400

commit v3 on v2

--- a/solution.py
+++ b/solution.py
@@ -117,9 +117,13 @@
 ):
     tm = lax.axis_index("tm")
     space = lax.axis_index("space")
+    row, col = lax.div(tm, near), lax.rem(tm, near)
 
     def at_tm(distance):
         return {"tm": lax.rem(tm + (distance + windows), windows)}
+
+    def at_place(other_row, other_col):
+        return {"tm": near * lax.rem(other_row + far, far) + lax.rem(other_col, near)}
 
     def at_space(distance):
         return {"space": lax.rem(space + (distance + parts), parts)}
@@ -132,7 +136,6 @@
         copy.start()
         return copy
 
-    sources = sorted(set(range(1, near + 1)) | {near * m for m in range(1, far)} | {windows - 1})
     barrier = pltpu.get_barrier_semaphore()
     for distance in (1, -1):
         pl.semaphore_signal(barrier, inc=1, device_id=at_space(distance), device_id_type=MESH)
@@ -149,8 +152,11 @@
         for load in loads[-1]:
             load.start()
 
-    for distance in sources:
-        pl.semaphore_signal(barrier, inc=1, device_id=at_tm(-distance), device_id_type=MESH)
+    targets = [at_place(row, col + m) for m in range(1, near)] + [at_place(row + m, col) for m in range(1, far)]
+    last = jnp.where(col == near - 1, 1, 0)
+    targets.append(at_place(row - 1 + 2 * last, (near - 1) * (1 - last)))
+    for target in targets:
+        pl.semaphore_signal(barrier, inc=1, device_id=target, device_id_type=MESH)
 
     def arrive(number):
         for load in loads[number]:
@@ -258,14 +264,13 @@
 
     copies = []
     right, left = halo_start(0, state)
-    pl.semaphore_wait(barrier, len(sources) + 2)
+    pl.semaphore_wait(barrier, near + far + jnp.where(col == 0, 1, 0) + (near - 1) * last)
     halo = halo_send(0)
     lifted[...] = jnp.zeros_like(lifted)
     arrive(3)
-    keep = jnp.where(tm == 0, 0.0, 1.0)
-    blocks[0] = coarse[...] * keep
+    blocks[pl.ds(col, 1)] = coarse[...][None]
     for m in range(1, near):
-        copies.append(send(blocks.at[0], blocks.at[m], block_sem, m, at_tm(m)))
+        copies.append(send(coarse, blocks.at[col], block_sem, m, at_place(row, col + m)))
     arrive(6)
     ends[...] = node_sum(lambda row, half: state[half, row : row + 64, :])
     end_copy = send(ends, ends_next, end_sem, 0, at_tm(-1))
@@ -293,6 +298,20 @@
     local_part(middle, right, left)
     for k in range(2, 6):
         align(k)
+    for copy in copies:
+        copy.wait()
+    columns = [column(blocks.at[0], g) for g in range(5)]
+    upto = columns
+    for m in range(1, near):
+        columns = [matvec(blocks.at[m], vector) for vector in columns]
+        upto = [jnp.where(col >= m, new, old) for new, old in zip(columns, upto)]
+    for slot, matrix in ((0, columns), (far - 1, upto)):
+        for g in range(5):
+            for half in range(2):
+                products[slot, pl.ds(2 * g + half, 5, stride=10), :] = matrix[g][:, 128 * half : 128 * half + 128]
+    copies = [
+        send(products.at[0], products.at[m], product_sem, m, at_place(row + m, col)) for m in range(1, far - 1)
+    ]
     for copy in halo:
         copy.wait()
     halo_part(1)
@@ -302,38 +321,52 @@
 
     end_copy.wait()
     coarse_out[...] = node_sum(lambda row, half: start[row : row + 64, 128 * half : 128 * half + 128]) - ends_next[...]
-    rounds = [send(coarse_out, coarse_in.at[m], coarse_sem, m, at_tm(m + 1)) for m in range(near)]
+    slot = lax.rem(col + 1, near)
+    rounds = [
+        send(coarse_out, coarse_in.at[slot], coarse_sem, m, at_place(row + last, col + 1 + m)) for m in range(near - 1)
+    ]
+    across = pltpu.make_async_remote_copy(
+        src_ref=coarse_out, dst_ref=coarse_in.at[slot], send_sem=coarse_sem.at[0, near - 1],
+        recv_sem=coarse_sem.at[1, near - 1], device_id=at_place(row + 1, near - 1), device_id_type=MESH,
+    )
+
+    @pl.when(last == 1)
+    def _():
+        across.start()
+
+    @pl.when(last == 0)
+    def _():
+        coarse_in[pl.ds(slot, 1)] = coarse_out[...][None]
+
     def bulk_send(fields):
         return [
             send(start.at[pl.ds(64 * f, 64)], shifted.at[pl.ds(64 * f, 64)], bulk_sem, f, at_tm(1)) for f in fields
         ]
 
     bulk = bulk_send(range(EARLY))
-    for copy in copies:
-        copy.wait()
-    columns = [column(blocks.at[near - 1], g) for g in range(5)]
-    for m in range(near - 2, -1, -1):
-        columns = [matvec(blocks.at[m], vector) for vector in columns]
-    for g in range(5):
-        for half in range(2):
-            products[0, pl.ds(2 * g + half, 5, stride=10), :] = columns[g][:, 128 * half : 128 * half + 128]
-    copies = [send(products.at[0], products.at[m], product_sem, m, at_tm(near * m)) for m in range(1, far - 1)]
     for copy in rounds:
         copy.wait()
-    vector = coarse_in[near - 1]
-    for m in range(near - 2, -1, -1):
+
+    @pl.when(last == 1)
+    def _():
+        across.wait()
+
+    vector = coarse_in[0]
+    inside = vector
+    for m in range(1, near):
         vector = coarse_in[m] + matvec(blocks.at[m], vector)
+        inside = jnp.where(col >= m, vector, inside)
     window_out[...] = vector
-    rounds = [send(window_out, window_in.at[m], window_sem, m, at_tm(near * m)) for m in range(1, far)]
+    rounds = [send(window_out, window_in.at[m], window_sem, m, at_place(row + m, col)) for m in range(1, far)]
     bulk += bulk_send(range(EARLY, FIELDS))
     for copy in copies:
         copy.wait()
     for copy in rounds:
         copy.wait()
-    vector = window_in[far - 1]
+    vector = jnp.where(row >= far - 1, window_in[far - 1], 0.0)
     for m in range(far - 2, 0, -1):
-        vector = window_in[m] + matvec(products.at[m], vector)
-    correction[...] = window_out[...] + matvec(products.at[0], vector)
+        vector = jnp.where(row >= m, window_in[m] + matvec(products.at[m], vector), 0.0)
+    correction[...] = inside + matvec(products.at[far - 1], vector)
     for copy in bulk:
         copy.wait()
 
@@ -377,7 +410,7 @@
                 pltpu.VMEM((2, 2, 80, SURFACE), f32),
                 pltpu.VMEM((2, 2, 80, SURFACE), f32),
                 pltpu.VMEM((near, 50, 128), f32),
-                pltpu.VMEM((max(far - 1, 1), 50, 128), f32),
+                pltpu.VMEM((far, 50, 128), f32),
                 pltpu.VMEM((5, ELEMS), f32),
                 pltpu.VMEM((5, ELEMS), f32),
                 pltpu.VMEM((5, ELEMS), f32),

time: 37.5 us -> 35.1 us (0.936)
  Pallas kernels: 35.7 us -> 33.3 us
    pallas_call x1, Pallas kernels: 35.7 us -> 33.3 us  [per_device(): pl.pallas_call(functools.partial(kernel, windows, parts, near, far), out_...]
where the time goes in v3:
time: 35.1 us; the launch traced here: 35 us
  Pallas kernels  33.3 us (95%)
  other arithmetic  1.73 us (5%)
    pallas_call x1, Pallas kernels, per_device(): pl.pallas_call(functools.partial(kernel, windows, parts, near, far), out_...  33.3 us
    add x1, other arithmetic, per_device(): shifted.reshape(1, FIELDS, NODES, ELEMS) + correction[None, :, None, :]  1.73 us

profile of v3, /device:TPU:1, one launch (start us, length us, event | category | flops | bytes accessed | tf_op | source)
XLA Modules:
  0.0 35.0 jit_solution(15167364973400931350)
XLA Ops:
  0.0 33.3 %shard_map.91 = (f32[320,256]{1,0:T(8,128)}, f32[5,256]{1,0:T(8,128)}) custom-call(f32[320,256]{1,0:T(8,128)} %bitcast.5, bf16[2,320,256]{2,1,0:T(8,128)(2,1)} %bitcast.6, f32[150,1,128]{2,1,0:T(1,128)} %bitcast.8, f32[50,1,128]{2,1,0:T(1,128)} %bitcast.9, s32[6,256]{1,0:T(8,128)} %neigh_hbm.1, s32[6,256]{1,0:T(8,128)} %orient_hbm.1, s32[2,128]{1,0:T(2,128)} %inter_hbm.1, ...), custom_call_target="tpu_custom_call" | custom-call | tf_op jit(solution)/shard_map/pallas_call | solution.py:393
  33.3 1.7 %broadcast_add_fusion = f32[1,5,64,256]{3,2,1,0:T(8,128)} fusion(f32[1,5,64,256]{3,2,1,0:T(8,128)} %bitcast.7, f32[5,256]{1,0:T(8,128)} %get-tuple-element.8), kind=kLoop, calls=%fused_computation | loop fusion | flops 81920 | bytes 660480 | tf_op jit(solution)/shard_map/add | solution.py:433

commit v4 on v3

--- a/solution.py
+++ b/solution.py
@@ -18,7 +18,6 @@
 SURFACE = 128
 STEP = 0.02
 LIFT = 3.0
-EARLY = 2
 bf16 = jnp.bfloat16
 f32 = jnp.float32
 
@@ -226,41 +225,62 @@
             total = wide(fetched, rows) + gathered(split(halo_in[turn, side]), chosen[...])
             store_wide(fetched, rows, total)
 
-    def store_middle(row, half, value):
-        middle[half, row : row + 32, :] = value
-
-    def store_start(row, half, value):
-        start[row : row + 32, 128 * half : 128 * half + 128] = value
-
-    def mix(values, source, store):
-        for group in range(2):
-            low = 32 * group
-            for half in range(2):
-                lanes = slice(128 * half, 128 * half + 128)
-                own = pat[64 + low : 96 + low, :]
-                totals = [
-                    own * values[half, 64 * f + low : 64 * f + low + 32, :]
-                    + forcing[source, 64 * f + low : 64 * f + low + 32, lanes].astype(f32)
-                    for f in range(FIELDS)
-                ]
-                for d in range(3):
-                    sign = pat[128 + 64 * d + low : 160 + 64 * d + low, :]
-                    for h in range(FIELDS):
-                        face = lifted[half, pl.ds((64 * d + low) * 8 + h, 32, stride=8), :]
-                        base = 192 * h + 64 * d + low
-                        term = terms[base : base + 32, lanes] + sign * face
+    def store_middle(field, low, count, half, value):
+        middle[half, 64 * field + low : 64 * field + low + count, :] = value
+
+    def store_start(field, low, count, half, value):
+        start[field, low : low + count, 128 * half : 128 * half + 128] = value
+
+    def mix(values, source, store, low, count):
+        for half in range(2):
+            lanes = slice(128 * half, 128 * half + 128)
+            own = pat[64 + low : 64 + low + count, :]
+            totals = [
+                own * values[half, 64 * f + low : 64 * f + low + count, :]
+                + forcing[source, 64 * f + low : 64 * f + low + count, lanes].astype(f32)
+                for f in range(FIELDS)
+            ]
+            for d in range(3):
+                sign = pat[128 + 64 * d + low : 128 + 64 * d + low + count, :]
+                for h in range(FIELDS):
+                    base = 192 * h + 64 * d + low
+                    term = terms[base : base + count, lanes]
+                    if d > 0 or low in (0, 48):
+                        face = lifted[half, pl.ds((64 * d + low) * 8 + h, count, stride=8), :]
+                        term = term + sign * face
                         totals[h] = totals[h] + face
-                        for f in range(FIELDS):
-                            totals[f] = totals[f] + jac[10 * (5 * d + h) + 2 * f + half : 10 * (5 * d + h) + 2 * f + half + 1, :] * term
-                for f in range(FIELDS):
-                    store(64 * f + low, half, totals[f])
-
-    def node_sum(piece):
+                    for f in range(FIELDS):
+                        number = 10 * (5 * d + h) + 2 * f + half
+                        totals[f] = totals[f] + jac[number : number + 1, :] * term
+            for f in range(FIELDS):
+                store(f, low, count, half, totals[f])
+
+    def inner(values, source, store):
+        mix(values, source, store, 16, 32)
+
+    def outer(values, source, store):
+        mix(values, source, store, 0, 16)
+        mix(values, source, store, 48, 16)
+
+    def node_sum(piece, low, count):
         sums = []
         for f in range(FIELDS):
-            halves = [jnp.sum(pat[0:64, :] * piece(64 * f, half), axis=0, keepdims=True) for half in range(2)]
+            halves = [
+                jnp.sum(pat[low : low + count, :] * piece(f, low, count, half), axis=0, keepdims=True)
+                for half in range(2)
+            ]
             sums.append(jnp.concatenate(halves, axis=1))
         return jnp.concatenate(sums, axis=0)
+
+    def state_piece(f, low, count, half):
+        return state[half, 64 * f + low : 64 * f + low + count, :]
+
+    def start_piece(f, low, count, half):
+        return start[f, low : low + count, 128 * half : 128 * half + 128]
+
+    def bulk_send(index, low, count):
+        rows = pl.ds(low, count)
+        return send(start.at[:, rows], shifted.at[:, rows], bulk_sem, index, at_tm(1))
 
     copies = []
     right, left = halo_start(0, state)
@@ -272,7 +292,7 @@
     for m in range(1, near):
         copies.append(send(coarse, blocks.at[col], block_sem, m, at_place(row, col + m)))
     arrive(6)
-    ends[...] = node_sum(lambda row, half: state[half, row : row + 64, :])
+    ends[...] = node_sum(state_piece, 0, 64)
     end_copy = send(ends, ends_next, end_sem, 0, at_tm(-1))
     arrive(2)
     for k in range(6):
@@ -284,20 +304,25 @@
     arrive(4)
     for k in range(2, 6):
         align(k)
+    arrive(7)
+    arrive(8)
+    inner(state, 1, store_middle)
     for copy in halo:
         copy.wait()
     halo_part(0)
     align(0)
     align(1)
-    arrive(7)
-    arrive(8)
-    mix(state, 1, store_middle)
+    outer(state, 1, store_middle)
 
     right, left = halo_start(1, middle)
     halo = halo_send(1)
     local_part(middle, right, left)
     for k in range(2, 6):
         align(k)
+    inner(middle, 0, store_start)
+    bulk = [bulk_send(0, 16, 32)]
+    end_copy.wait()
+    coarse_out[...] = node_sum(start_piece, 16, 32) - ends_next[...]
     for copy in copies:
         copy.wait()
     columns = [column(blocks.at[0], g) for g in range(5)]
@@ -317,10 +342,8 @@
     halo_part(1)
     align(0)
     align(1)
-    mix(middle, 0, store_start)
-
-    end_copy.wait()
-    coarse_out[...] = node_sum(lambda row, half: start[row : row + 64, 128 * half : 128 * half + 128]) - ends_next[...]
+    outer(middle, 0, store_start)
+    coarse_out[...] = coarse_out[...] + node_sum(start_piece, 0, 16) + node_sum(start_piece, 48, 16)
     slot = lax.rem(col + 1, near)
     rounds = [
         send(coarse_out, coarse_in.at[slot], coarse_sem, m, at_place(row + last, col + 1 + m)) for m in range(near - 1)
@@ -338,12 +361,7 @@
     def _():
         coarse_in[pl.ds(slot, 1)] = coarse_out[...][None]
 
-    def bulk_send(fields):
-        return [
-            send(start.at[pl.ds(64 * f, 64)], shifted.at[pl.ds(64 * f, 64)], bulk_sem, f, at_tm(1)) for f in fields
-        ]
-
-    bulk = bulk_send(range(EARLY))
+    bulk += [bulk_send(1, 0, 16), bulk_send(2, 48, 16)]
     for copy in rounds:
         copy.wait()
 
@@ -358,7 +376,6 @@
         inside = jnp.where(col >= m, vector, inside)
     window_out[...] = vector
     rounds = [send(window_out, window_in.at[m], window_sem, m, at_place(row + m, col)) for m in range(1, far)]
-    bulk += bulk_send(range(EARLY, FIELDS))
     for copy in copies:
         copy.wait()
     for copy in rounds:
@@ -392,9 +409,9 @@
         )
         shifted, correction = pl.pallas_call(
             functools.partial(kernel, windows, parts, near, far),
-            out_shape=(jax.ShapeDtypeStruct((ROWS, ELEMS), f32), jax.ShapeDtypeStruct((FIELDS, ELEMS), f32)),
+            out_shape=(pltpu.VMEM((FIELDS, NODES, ELEMS), f32), pltpu.VMEM((FIELDS, ELEMS), f32)),
             in_specs=[pl.BlockSpec(memory_space=pl.ANY)] * len(operands),
-            out_specs=(pl.BlockSpec(memory_space=pl.ANY), pl.BlockSpec(memory_space=pltpu.VMEM)),
+            out_specs=(pl.BlockSpec(memory_space=pltpu.VMEM), pl.BlockSpec(memory_space=pltpu.VMEM)),
             scratch_shapes=[pltpu.VMEM((2, ROWS, 128), f32)]
             + [pltpu.VMEM((x.shape[0], 128) if x.shape[1] == 1 else x.shape, x.dtype) for x in operands[1:]]
             + [
@@ -406,7 +423,7 @@
                 pltpu.VMEM((2, 3 * 64 * 8, 128), f32),
                 pltpu.VMEM((15 * 64, ELEMS), f32),
                 pltpu.VMEM((2, ROWS, 128), f32),
-                pltpu.VMEM((ROWS, ELEMS), f32),
+                pltpu.VMEM((FIELDS, NODES, ELEMS), f32),
                 pltpu.VMEM((2, 2, 80, SURFACE), f32),
                 pltpu.VMEM((2, 2, 80, SURFACE), f32),
                 pltpu.VMEM((near, 50, 128), f32),
@@ -424,13 +441,13 @@
                 dma((2, 1)),
                 dma((2, near)),
                 dma((2, far)),
-                dma((2, 5)),
+                dma((2, 3)),
             ],
             compiler_params=pltpu.CompilerParams(
                 collective_id=0, has_side_effects=True, vmem_limit_bytes=60 * 2**20
             ),
         )(*operands)
-        return shifted.reshape(1, FIELDS, NODES, ELEMS) + correction[None, :, None, :]
+        return shifted[None] + correction[None, :, None, :]
 
     in_specs = (
         P("tm", None, None, "space"),

time: 35.1 us -> 31.5 us (0.90)
  Pallas kernels: 33.3 us -> 30.7 us
  other arithmetic: 1.73 us -> 0.75 us
    pallas_call x1, Pallas kernels: 33.3 us -> 30.7 us  [per_device(): pl.pallas_call(functools.partial(kernel, windows, parts, near, far), out_...]
    add x1, other arithmetic: 1.73 us -> 0.75 us  [per_device(): return shifted[None] + correction[None, :, None, :]]
where the time goes in v4:
time: 31.5 us
  Pallas kernels  30.7 us (97%)
  other arithmetic  0.75 us (2%)
    pallas_call x1, Pallas kernels, per_device(): pl.pallas_call(functools.partial(kernel, windows, parts, near, far), out_...  30.7 us
    add x1, other arithmetic, per_device(): return shifted[None] + correction[None, :, None, :]  0.75 us

profile of v4, /device:TPU:1, one launch (start us, length us, event | category | flops | bytes accessed | tf_op | source)
XLA Modules:
  0.0 31.5 jit_solution(10280737091850309351)
XLA Ops:
  0.0 30.7 %shard_map.91 = (f32[5,64,256]{2,1,0:T(8,128)S(1)}, f32[5,256]{1,0:T(8,128)S(1)}) custom-call(f32[320,256]{1,0:T(8,128)} %bitcast.6, bf16[2,320,256]{2,1,0:T(8,128)(2,1)} %bitcast.7, f32[150,1,128]{2,1,0:T(1,128)} %bitcast.8, f32[50,1,128]{2,1,0:T(1,128)} %bitcast.9, s32[6,256]{1,0:T(8,128)} %neigh_hbm.1, s32[6,256]{1,0:T(8,128)} %orient_hbm.1, ...), custom_call_target="tpu_custom_call" | custom-call | tf_op jit(solution)/shard_map/pallas_call | solution.py:410
  30.7 0.8 %add_bitcast_fusion = f32[1,5,64,256]{3,2,1,0:T(8,128)} fusion(f32[5,64,256]{2,1,0:T(8,128)S(1)} %get-tuple-element.7, f32[5,256]{1,0:T(8,128)S(1)} %get-tuple-element.8), kind=kLoop, calls=%fused_computation | loop fusion | flops 81920 | bytes 660480 | tf_op jit(solution)/shard_map/add | solution.py:450

commit v5 on v4

--- a/solution.py
+++ b/solution.py
@@ -138,6 +138,26 @@
     barrier = pltpu.get_barrier_semaphore()
     for distance in (1, -1):
         pl.semaphore_signal(barrier, inc=1, device_id=at_space(distance), device_id_type=MESH)
+    def down_copy(src, dst, sems, m):
+        return pltpu.make_async_remote_copy(
+            src_ref=src, dst_ref=dst, send_sem=sems.at[0, m], recv_sem=sems.at[1, m],
+            device_id=at_place(row + m, col), device_id_type=MESH,
+        )
+
+    def down(src, dst, sems, m):
+        @pl.when(row + m < far)
+        def _():
+            down_copy(src, dst, sems, m).start()
+
+    def down_wait(src, dst, sems, m):
+        @pl.when(row + m < far)
+        def _():
+            down_copy(src, dst, sems, m).wait_send()
+
+        @pl.when(row >= m)
+        def _():
+            down_copy(src, dst, sems, m).wait_recv()
+
     loads = []
     for number, (src, dst) in enumerate([
         (inter_hbm, inter), (state_hbm, state), (neigh_hbm, neigh), (coarse_hbm.at[:, 0, :], coarse),
@@ -334,9 +354,19 @@
         for g in range(5):
             for half in range(2):
                 products[slot, pl.ds(2 * g + half, 5, stride=10), :] = matrix[g][:, 128 * half : 128 * half + 128]
-    copies = [
-        send(products.at[0], products.at[m], product_sem, m, at_place(row + m, col)) for m in range(1, far - 1)
-    ]
+    for m in range(1, far - 1):
+        down(products.at[0], products.at[m], product_sem, m)
+
+        @pl.when(row < m)
+        def _():
+            products[m] = jnp.zeros((50, 128), f32)
+
+    for m in range(1, far):
+
+        @pl.when(row < m)
+        def _():
+            window_in[m] = jnp.zeros((FIELDS, ELEMS), f32)
+
     for copy in halo:
         copy.wait()
     halo_part(1)
@@ -375,14 +405,15 @@
         vector = coarse_in[m] + matvec(blocks.at[m], vector)
         inside = jnp.where(col >= m, vector, inside)
     window_out[...] = vector
-    rounds = [send(window_out, window_in.at[m], window_sem, m, at_place(row + m, col)) for m in range(1, far)]
-    for copy in copies:
-        copy.wait()
-    for copy in rounds:
-        copy.wait()
-    vector = jnp.where(row >= far - 1, window_in[far - 1], 0.0)
+    for m in range(1, far):
+        down(window_out, window_in.at[m], window_sem, m)
+    for m in range(1, far - 1):
+        down_wait(products.at[0], products.at[m], product_sem, m)
+    for m in range(1, far):
+        down_wait(window_out, window_in.at[m], window_sem, m)
+    vector = window_in[far - 1]
     for m in range(far - 2, 0, -1):
-        vector = jnp.where(row >= m, window_in[m] + matvec(products.at[m], vector), 0.0)
+        vector = window_in[m] + matvec(products.at[m], vector)
     correction[...] = inside + matvec(products.at[far - 1], vector)
     for copy in bulk:
         copy.wait()

time: 31.5 us -> 28 us (0.89)
  Pallas kernels: 30.7 us -> 27.1 us
    pallas_call x1, Pallas kernels: 30.7 us -> 27.1 us  [per_device(): pl.pallas_call(functools.partial(kernel, windows, parts, near, far), out_...]
where the time goes in v5:
time: 28 us; the launch traced here: 27.8 us
  Pallas kernels  27.1 us (97%)
  other arithmetic  0.75 us (3%)
    pallas_call x1, Pallas kernels, per_device(): pl.pallas_call(functools.partial(kernel, windows, parts, near, far), out_...  27.1 us
    add x1, other arithmetic, per_device(): return shifted[None] + correction[None, :, None, :]  0.75 us

profile of v5, /device:TPU:1, one launch (start us, length us, event | category | flops | bytes accessed | tf_op | source)
XLA Modules:
  0.0 27.8 jit_solution(16037619298646876204)
XLA Ops:
  0.0 27.1 %shard_map.91 = (f32[5,64,256]{2,1,0:T(8,128)S(1)}, f32[5,256]{1,0:T(8,128)S(1)}) custom-call(f32[320,256]{1,0:T(8,128)} %bitcast.6, bf16[2,320,256]{2,1,0:T(8,128)(2,1)} %bitcast.7, f32[150,1,128]{2,1,0:T(1,128)} %bitcast.8, f32[50,1,128]{2,1,0:T(1,128)} %bitcast.9, s32[6,256]{1,0:T(8,128)} %neigh_hbm.1, s32[6,256]{1,0:T(8,128)} %orient_hbm.1, ...), custom_call_target="tpu_custom_call" | custom-call | tf_op jit(solution)/shard_map/pallas_call | solution.py:441
  27.1 0.8 %add_bitcast_fusion = f32[1,5,64,256]{3,2,1,0:T(8,128)} fusion(f32[5,64,256]{2,1,0:T(8,128)S(1)} %get-tuple-element.7, f32[5,256]{1,0:T(8,128)S(1)} %get-tuple-element.8), kind=kLoop, calls=%fused_computation | loop fusion | flops 81920 | bytes 660480 | tf_op jit(solution)/shard_map/add | solution.py:481

commit v6 on v5

--- a/solution.py
+++ b/solution.py
@@ -144,17 +144,17 @@
             device_id=at_place(row + m, col), device_id_type=MESH,
         )
 
-    def down(src, dst, sems, m):
-        @pl.when(row + m < far)
+    def down(src, dst, sems, m, first=0):
+        @pl.when((row >= first) & (row + m < far))
         def _():
             down_copy(src, dst, sems, m).start()
 
-    def down_wait(src, dst, sems, m):
-        @pl.when(row + m < far)
+    def down_wait(src, dst, sems, m, first=0):
+        @pl.when((row >= first) & (row + m < far))
         def _():
             down_copy(src, dst, sems, m).wait_send()
 
-        @pl.when(row >= m)
+        @pl.when(row >= m + first)
         def _():
             down_copy(src, dst, sems, m).wait_recv()
 
@@ -202,9 +202,11 @@
             send(halo_out.at[turn, 1], halo_in.at[turn, 1], halo_sem, 2 * turn + 1, at_space(-1)),
         ]
 
-    def local_part(values, right, left):
+    def local_x(right, left):
         store_wide(fetched, pl.ds(0, 80), gathered(right, hot[0]))
         store_wide(fetched, pl.ds(160, 80), gathered(left, hot[1]))
+
+    def local_part(values):
         for k in (2, 3):
             low = 8 if k == 2 else 0
             starts = [64 * f + 16 * a + low for f in range(FIELDS) for a in range(4)]
@@ -320,13 +322,14 @@
     hot_left[...] = one_hot(neigh[0:1, :], ELEMS, SURFACE)
     hot_right[...] = one_hot(neigh[1:2, :], ELEMS + SURFACE, SURFACE)
     arrive(5)
-    local_part(state, right, left)
+    local_part(state)
     arrive(4)
     for k in range(2, 6):
         align(k)
     arrive(7)
     arrive(8)
     inner(state, 1, store_middle)
+    local_x(right, left)
     for copy in halo:
         copy.wait()
     halo_part(0)
@@ -336,11 +339,12 @@
 
     right, left = halo_start(1, middle)
     halo = halo_send(1)
-    local_part(middle, right, left)
+    local_part(middle)
     for k in range(2, 6):
         align(k)
     inner(middle, 0, store_start)
     bulk = [bulk_send(0, 16, 32)]
+    local_x(right, left)
     end_copy.wait()
     coarse_out[...] = node_sum(start_piece, 16, 32) - ends_next[...]
     for copy in copies:
@@ -355,9 +359,9 @@
             for half in range(2):
                 products[slot, pl.ds(2 * g + half, 5, stride=10), :] = matrix[g][:, 128 * half : 128 * half + 128]
     for m in range(1, far - 1):
-        down(products.at[0], products.at[m], product_sem, m)
-
-        @pl.when(row < m)
+        down(products.at[0], products.at[m], product_sem, m, 1)
+
+        @pl.when(row < m + 1)
         def _():
             products[m] = jnp.zeros((50, 128), f32)
 
@@ -408,7 +412,7 @@
     for m in range(1, far):
         down(window_out, window_in.at[m], window_sem, m)
     for m in range(1, far - 1):
-        down_wait(products.at[0], products.at[m], product_sem, m)
+        down_wait(products.at[0], products.at[m], product_sem, m, 1)
     for m in range(1, far):
         down_wait(window_out, window_in.at[m], window_sem, m)
     vector = window_in[far - 1]

time: 28 us -> 27.9 us (level)
  no operation moved by 1% of the time
where the time goes in v6:
time: 27.9 us; the launch traced here: 27.6 us
  Pallas kernels  26.9 us (96%)
  other arithmetic  0.75 us (3%)
    pallas_call x1, Pallas kernels, per_device(): pl.pallas_call(functools.partial(kernel, windows, parts, near, far), out_...  26.9 us
    add x1, other arithmetic, per_device(): return shifted[None] + correction[None, :, None, :]  0.75 us

profile of v6, /device:TPU:1, one launch (start us, length us, event | category | flops | bytes accessed | tf_op | source)
XLA Modules:
  0.0 27.6 jit_solution(12723391571772981930)
XLA Ops:
  0.0 26.9 %shard_map.91 = (f32[5,64,256]{2,1,0:T(8,128)S(1)}, f32[5,256]{1,0:T(8,128)S(1)}) custom-call(f32[320,256]{1,0:T(8,128)} %bitcast.6, bf16[2,320,256]{2,1,0:T(8,128)(2,1)} %bitcast.7, f32[150,1,128]{2,1,0:T(1,128)} %bitcast.8, f32[50,1,128]{2,1,0:T(1,128)} %bitcast.9, s32[6,256]{1,0:T(8,128)} %neigh_hbm.1, s32[6,256]{1,0:T(8,128)} %orient_hbm.1, ...), custom_call_target="tpu_custom_call" | custom-call | tf_op jit(solution)/shard_map/pallas_call | solution.py:445
  26.9 0.8 %add_bitcast_fusion = f32[1,5,64,256]{3,2,1,0:T(8,128)} fusion(f32[5,64,256]{2,1,0:T(8,128)S(1)} %get-tuple-element.7, f32[5,256]{1,0:T(8,128)S(1)} %get-tuple-element.8), kind=kLoop, calls=%fused_computation | loop fusion | flops 81920 | bytes 660480 | tf_op jit(solution)/shard_map/add | solution.py:485
